TPU v7x, 512 devices: a whole 4x8x8 slice. The times are simulated.
512 devices in a mesh: row: 32 (over y, z_lo), col: 16 (over z_hi, x, core).
Axes of the slice: x: 4, y: 8, z: 8 (z_hi: 2, z_lo: 4; z = z_hi * 4 + z_lo), core: 2. Of those that a mesh axis runs over, the one named last changes fastest.
Arguments:
- embeddings: bfloat16 [8192, 256], P(('row', 'col')), may hold values from -6 to 6
- labels: bfloat16 [8192, 1024], P(('row', 'col')), may hold values from -6 to 6
- tile_mask: int32 [32, 32], replicated, may hold values 0 or 1
Outputs:
- spread_labels: bfloat16 [8192, 1024], P(('row', 'col'))
Inputs may be any that keep to these rules, and one draw needn't show every extreme that they name: Only the entries tile_mask[i, j] with i < j are read; the tile of blocks i and j (and of j and i) is kept where it is 1.
All inputs are finite; a program needn't handle non-finite values.
Results may differ from a plain program's by a relative error of at most 0.015.
Values may be sent and summed in bfloat16 or wider, within the bound.
A program may use at most 64 MiB of HBM per device.

v0:
```python
import math

import jax
import jax.numpy as jnp
from jax import lax
from jax.sharding import PartitionSpec as P

BLOCK = 256
ITERS = 2


MIXING = 0.9
SHARPNESS = 3.0
EPSILON = 1e-06


def unit_rows(embeddings):
    values = embeddings.astype(jnp.float32)
    return (values * lax.rsqrt(jnp.sum(values * values, axis=1, keepdims=True) + EPSILON)).astype(
        jnp.bfloat16
    )


def symmetric_keep(tile_mask):
    blocks = tile_mask.shape[0]
    block_row = lax.broadcasted_iota(jnp.int32, (blocks, blocks), 0)
    block_col = lax.broadcasted_iota(jnp.int32, (blocks, blocks), 1)
    mirrored = jnp.where(block_row < block_col, tile_mask, tile_mask.T)
    return (jnp.where(block_row == block_col, 1, mirrored), block_row, block_col)


def rotate_rows(values, start):
    total = values.shape[0]
    doubled = jnp.concatenate([values, values], axis=0)
    return lax.dynamic_slice_in_dim(doubled, start, total, 0)


def both_terms(operands):
    row_kernel, col_kernel, part_labels, row_labels = operands
    row_term = jnp.dot(row_kernel, part_labels, preferred_element_type=jnp.float32)
    col_term = lax.dot_general(
        col_kernel, row_labels, (((0,), (0,)), ((), ())), preferred_element_type=jnp.float32
    )
    return (row_term, col_term)


def no_terms(operands):
    row_kernel, col_kernel, part_labels, row_labels = operands
    return (
        jnp.zeros((row_kernel.shape[0], part_labels.shape[1]), jnp.float32),
        jnp.zeros((col_kernel.shape[1], row_labels.shape[1]), jnp.float32),
    )


def shards(embeddings, labels, tile_mask):
    row_count = lax.axis_size("row")
    col_count = lax.axis_size("col")
    row_index = lax.axis_index("row")
    col_index = lax.axis_index("col")
    piece_rows = embeddings.shape[0]
    emb_width = embeddings.shape[1]
    channels = labels.shape[1]
    blocks = tile_mask.shape[0]
    sharpness = SHARPNESS * math.sqrt(emb_width)
    unit_vecs = unit_rows(embeddings)
    row_units = lax.all_gather(unit_vecs, "col", axis=0, tiled=True)
    col_gathered = lax.all_gather(unit_vecs, "row", axis=0, tiled=True)
    row_total = row_units.shape[0]
    col_total = col_gathered.shape[0]
    shift = row_index * piece_rows
    back_shift = col_total - shift
    col_units = rotate_rows(col_gathered, shift)
    unit_count = math.gcd(8, row_count)
    unit_width = col_total // unit_count
    kept_sym, block_row, block_col = symmetric_keep(tile_mask)
    chosen = block_row <= block_col
    tile_table = jnp.where(chosen, kept_sym, 0)
    global_rows = row_index * row_total + jnp.arange(row_total, dtype=jnp.int32)
    row_blocks = global_rows // BLOCK
    block_ids = jnp.arange(blocks, dtype=jnp.int32)
    row_onehot = (row_blocks[:, None] == block_ids[None, :]).astype(jnp.bfloat16)
    row_table = jnp.dot(
        row_onehot, tile_table.astype(jnp.bfloat16), preferred_element_type=jnp.float32
    ).astype(jnp.bfloat16)
    local_cols = (jnp.arange(col_total, dtype=jnp.int32) + shift) % col_total
    global_cols = (
        local_cols // piece_rows * col_count + col_index
    ) * piece_rows + local_cols % piece_rows
    col_blocks = global_cols // BLOCK
    kernels_row = []
    kernels_col = []
    active_flags = []
    col_degree = []
    row_degree = jnp.zeros((row_total,), jnp.float32)
    for column_unit in range(unit_count):
        offset_cols = column_unit * unit_width
        part_units = col_units[offset_cols : offset_cols + unit_width]
        part_blocks = col_blocks[offset_cols : offset_cols + unit_width]
        part_cols = global_cols[offset_cols : offset_cols + unit_width]
        col_onehot = (part_blocks[:, None] == block_ids[None, :]).astype(jnp.bfloat16)
        kept_mask = lax.dot_general(
            row_table, col_onehot, (((1,), (1,)), ((), ())), preferred_element_type=jnp.float32
        )
        cosine = lax.dot_general(
            row_units, part_units, (((1,), (1,)), ((), ())), preferred_element_type=jnp.float32
        )
        distinct = global_rows[:, None] != part_cols[None, :]
        weights = jnp.where(
            distinct, jnp.exp(sharpness * cosine) * kept_mask, jnp.zeros_like(cosine)
        ).astype(jnp.bfloat16)
        active_flags.append(jnp.sum(kept_mask) > 0.0)
        kernels_row.append(weights)
        row_degree = row_degree + jnp.sum(weights, axis=1, dtype=jnp.float32)
        crossing = jnp.where(
            row_blocks[:, None] != part_blocks[None, :], weights, jnp.zeros_like(weights)
        )
        kernels_col.append(crossing)
        col_degree.append(jnp.sum(crossing, axis=0, dtype=jnp.float32))
    degree = lax.psum_scatter(row_degree, "col", scatter_dimension=0, tiled=True)
    col_sums = rotate_rows(jnp.concatenate(col_degree), back_shift)
    degree = degree + lax.psum_scatter(col_sums, "row", scatter_dimension=0, tiled=True)
    inv_root = lax.rsqrt(degree)
    seed_scores = labels.astype(jnp.float32)
    current = seed_scores
    for iteration in range(ITERS):
        scaled = (inv_root[:, None] * current).astype(jnp.bfloat16)
        col_labels = rotate_rows(lax.all_gather(scaled, "row", axis=0, tiled=True), shift)
        row_sum = jnp.zeros((row_total, channels), jnp.float32)
        col_parts = []
        row_labels = lax.all_gather(scaled, "col", axis=0, tiled=True)
        for column_unit in range(unit_count):
            offset_cols = column_unit * unit_width
            part_labels = col_labels[offset_cols : offset_cols + unit_width]
            row_term, col_term = lax.cond(
                active_flags[column_unit],
                both_terms,
                no_terms,
                (kernels_row[column_unit], kernels_col[column_unit], part_labels, row_labels),
            )
            row_sum = row_sum + row_term
            col_parts.append(col_term)
        sent_rows = row_sum.astype(jnp.bfloat16).reshape(col_count, piece_rows, channels)
        arrived = lax.all_to_all(sent_rows, "col", split_axis=0, concat_axis=0, tiled=True)
        spread = jnp.sum(arrived, axis=0, dtype=jnp.float32)
        ordered = rotate_rows(jnp.concatenate(col_parts).astype(jnp.bfloat16), back_shift)
        sent_cols = ordered.reshape(row_count, piece_rows, channels)
        returned = lax.all_to_all(sent_cols, "row", split_axis=0, concat_axis=0, tiled=True)
        spread = spread + jnp.sum(returned, axis=0, dtype=jnp.float32)
        current = MIXING * inv_root[:, None] * spread + (1.0 - MIXING) * seed_scores
    return current.astype(jnp.bfloat16)


def solution(mesh):
    placed = (P(("row", "col"), None), P(("row", "col"), None), P())
    return jax.shard_map(
        shards, mesh=mesh, in_specs=placed, out_specs=P(("row", "col"), None), check_vma=False
    )
```

profile of v0, /device:TPU:1, one launch (start us, length us, event | category | flops | bytes accessed | tf_op | source)
XLA Modules:
  0.0 720.3 jit_solution(1597081947624436445)
XLA Ops:
  8.1 36.6 %all_gather.18 = bf16[256,256]{1,0:T(8,128)(2,1)S(1)} all-gather(bf16[16,256]{1,0:T(8,128)(2,1)S(1)} %fusion.91), channel_id=1, replica_groups=mesh['row'=32,'col'=16] {'col'}, dimensions={0}, use_global_device_ids=true | all-gather | bytes 139264 | tf_op jit(solution)/shard_map/all_gather | solution.py:66
  44.7 66.2 %all_gather.19 = bf16[512,256]{1,0:T(8,128)(2,1)S(1)} all-gather(bf16[16,256]{1,0:T(8,128)(2,1)S(1)} %fusion.91), channel_id=1, replica_groups=mesh['row'=32,'col'=16] {'row'}, dimensions={0}, use_global_device_ids=true | all-gather | bytes 270336 | tf_op jit(solution)/shard_map/all_gather | solution.py:67
  110.9 1.3 dynamic-slice.2
  112.2 1.3 dynamic-slice
  115.6 1.0 convolution_convert_fusion.16
  116.6 0.9 fusion.121
  118.3 0.9 fusion.123
  119.9 0.8 fusion.125
  120.8 0.8 fusion.126
  121.6 0.8 fusion.128
  122.4 0.9 fusion.127
  125.4 1.2 convert_reduce_fusion.4
  126.8 60.7 %all-reduce.1 = f32[512]{0:T(512)S(1)} all-reduce(f32[512]{0:T(512)S(1)} %dynamic_slice.19), channel_id=3, replica_groups=mesh['row'=32,'col'=16] {'row'}, use_global_device_ids=true, to_apply=%region_18.19.clone | all-reduce | flops 512 | bytes 4096
  187.4 70.1 %all-reduce = f32[256]{0:T(256)S(1)} all-reduce(f32[256]{0:T(256)S(1)} %add_add_fusion), channel_id=2, replica_groups=mesh['row'=32,'col'=16] {'col'}, use_global_device_ids=true, to_apply=%region_9.10.clone | all-reduce | flops 256 | bytes 2048
  263.4 26.8 %all_gather.21 = bf16[256,1024]{1,0:T(8,128)(2,1)S(1)} all-gather(bf16[16,1024]{1,0:T(8,128)(2,1)} %fusion.72), channel_id=1, replica_groups=mesh['row'=32,'col'=16] {'col'}, dimensions={0}, use_global_device_ids=true | all-gather | bytes 557056 | tf_op jit(solution)/shard_map/all_gather | solution.py:130
  290.2 90.9 %all-gather.3.cloned.1.call-done = bf16[512,1024]{1,0:T(8,128)(2,1)} async-done(((bf16[16,1024]{1,0:T(8,128)(2,1)}), bf16[512,1024]{1,0:T(8,128)(2,1)}) %all-gather.3.cloned.1.call-update) | async-done | bytes 1048592 | tf_op jit(solution)/shard_map/all_gather | solution.py:127
  381.0 2.0 fusion.65
  383.1 1.3 conditional.16
  383.1 1.0 convolution_convert_fusion
  385.0 1.0 copy-done
  386.5 0.9 copy-done.1
  388.1 0.9 copy-done.2
  389.6 1.0 copy-done.3
  391.1 1.0 copy-done.4
  392.1 2.0 conditional.22
  392.1 1.0 convolution_convert_fusion.6
  393.1 1.1 fusion.12
  394.2 1.0 copy-done.5
  395.1 3.7 conditional.23
  395.1 1.6 convolution_convert_fusion.7
  396.7 2.1 fusion.14
  398.8 4.7 add_convert_fusion.1
  403.5 31.6 %all-to-all-start = ((bf16[16,16,1024]{2,1,0:T(8,128)(2,1)}), bf16[16,16,1024]{2,1,0:T(8,128)(2,1)S(1)}, u32[]{:S(2)}, u32[]{:S(2)}) async-start(bf16[16,16,1024]{2,1,0:T(8,128)(2,1)} %bitcast.1), calls=%async_computation | async-start | bytes 1048576 | tf_op jit(solution)/shard_map/all_to_all | solution.py:143
  435.2 0.9 constant_dynamic-update-slice_fusion.8
  436.2 0.9 constant_dynamic-update-slice_fusion
  437.1 1.1 constant_dynamic-slice_fusion.1
  438.2 12.0 %all-to-all-done = bf16[16,16,1024]{2,1,0:T(8,128)(2,1)S(1)} async-done(((bf16[16,16,1024]{2,1,0:T(8,128)(2,1)}), bf16[16,16,1024]{2,1,0:T(8,128)(2,1)S(1)}, u32[]{:S(2)}, u32[]{:S(2)}) %all-to-all-start) | async-done | bytes 524320 | tf_op jit(solution)/shard_map/all_to_all | solution.py:143
  450.2 4.2 all-to-all-start.1
  454.5 27.0 %all-to-all-done.1 = bf16[32,16,1024]{2,1,0:T(8,128)(2,1)S(1)} async-done(((bf16[32,16,1024]{2,1,0:T(8,128)(2,1)}), bf16[32,16,1024]{2,1,0:T(8,128)(2,1)S(1)}, u32[]{:S(2)}, u32[]{:S(2)}) %all-to-all-start.1) | async-done | bytes 1048608 | tf_op jit(solution)/shard_map/all_to_all | solution.py:147
  482.4 34.1 %all_gather.23 = bf16[256,1024]{1,0:T(8,128)(2,1)S(1)} all-gather(bf16[16,1024]{1,0:T(8,128)(2,1)} %fusion.70), channel_id=1, replica_groups=mesh['row'=32,'col'=16] {'col'}, dimensions={0}, use_global_device_ids=true | all-gather | bytes 557056 | tf_op jit(solution)/shard_map/all_gather | solution.py:130
  516.5 94.4 %all-gather.5.cloned.1.call-done = bf16[512,1024]{1,0:T(8,128)(2,1)} async-done(((bf16[16,1024]{1,0:T(8,128)(2,1)}), bf16[512,1024]{1,0:T(8,128)(2,1)}) %all-gather.5.cloned.1.call-update) | async-done | bytes 1048592 | tf_op jit(solution)/shard_map/all_gather | solution.py:127
  610.9 2.0 fusion.64
  613.0 1.3 conditional.24
  613.0 1.0 convolution_convert_fusion.8
  615.6 0.9 copy-done.6
  617.2 1.0 copy-done.7
  618.7 1.0 copy-done.8
  620.2 1.0 copy-done.9
  621.7 1.0 copy-done.10
  622.7 2.0 conditional.30
  622.7 1.0 convolution_convert_fusion.14
  623.7 1.1 fusion.28
  624.8 1.0 copy-done.11
  625.8 3.7 conditional.31
  625.8 1.6 convolution_convert_fusion.15
  627.4 2.1 fusion.30
  629.5 4.7 add_convert_fusion
  634.1 32.0 %all-to-all-start.2 = ((bf16[16,16,1024]{2,1,0:T(8,128)(2,1)}), bf16[16,16,1024]{2,1,0:T(8,128)(2,1)S(1)}, u32[]{:S(2)}, u32[]{:S(2)}) async-start(bf16[16,16,1024]{2,1,0:T(8,128)(2,1)} %bitcast.3), calls=%async_computation.2 | async-start | bytes 1048576 | tf_op jit(solution)/shard_map/all_to_all | solution.py:143
  666.3 0.9 constant_dynamic-update-slice_fusion.24
  667.3 0.9 constant_dynamic-update-slice_fusion.16
  668.2 1.1 constant_dynamic-slice_fusion
  669.3 12.0 %all-to-all-done.2 = bf16[16,16,1024]{2,1,0:T(8,128)(2,1)S(1)} async-done(((bf16[16,16,1024]{2,1,0:T(8,128)(2,1)}), bf16[16,16,1024]{2,1,0:T(8,128)(2,1)S(1)}, u32[]{:S(2)}, u32[]{:S(2)}) %all-to-all-start.2) | async-done | bytes 524320 | tf_op jit(solution)/shard_map/all_to_all | solution.py:143
  681.3 4.2 all-to-all-start.3
  685.6 27.0 %all-to-all-done.3 = bf16[32,16,1024]{2,1,0:T(8,128)(2,1)S(1)} async-done(((bf16[32,16,1024]{2,1,0:T(8,128)(2,1)}), bf16[32,16,1024]{2,1,0:T(8,128)(2,1)S(1)}, u32[]{:S(2)}, u32[]{:S(2)}) %all-to-all-start.3) | async-done | bytes 1048608 | tf_op jit(solution)/shard_map/all_to_all | solution.py:147
  (157 shorter events, 21.4 us)
Async XLA Ops:
  6.5 374.5 %all-gather.3.cloned.1.call-start = ((), (), s32[]{:S(2)}) async-start(), calls=%async_computation.4 | async-start | bytes 1081344 | tf_op jit(solution)/shard_map/all_gather | solution.py:127
  118.3 139.4 %copy-start.25 = (bf16[16,1024]{1,0:T(8,128)(2,1)S(1)}, bf16[16,1024]{1,0:T(8,128)(2,1)}, u32[]{:S(2)}) copy-start(bf16[16,1024]{1,0:T(8,128)(2,1)} %param.36) | copy-start | bytes 98308
  124.1 2.5 copy-start.12
  124.3 265.3 %copy-start.13 = (bf16[256,64]{0,1:T(8,128)(2,1)}, bf16[256,64]{0,1:T(8,128)(2,1)S(1)}, u32[]{:S(2)}) copy-start(bf16[256,64]{0,1:T(8,128)(2,1)S(1)} %fusion.58) | copy-start | bytes 98308
  124.5 263.5 %copy-start.15 = (bf16[256,64]{0,1:T(8,128)(2,1)}, bf16[256,64]{0,1:T(8,128)(2,1)S(1)}, u32[]{:S(2)}) copy-start(bf16[256,64]{0,1:T(8,128)(2,1)S(1)} %fusion.59) | copy-start | bytes 98308
  124.7 261.8 %copy-start.17 = (bf16[256,64]{0,1:T(8,128)(2,1)}, bf16[256,64]{0,1:T(8,128)(2,1)S(1)}, u32[]{:S(2)}) copy-start(bf16[256,64]{0,1:T(8,128)(2,1)S(1)} %fusion.60) | copy-start | bytes 98308
  125.0 260.0 %copy-start.19 = (bf16[256,64]{0,1:T(8,128)(2,1)}, bf16[256,64]{0,1:T(8,128)(2,1)S(1)}, u32[]{:S(2)}) copy-start(bf16[256,64]{0,1:T(8,128)(2,1)S(1)} %fusion.61) | copy-start | bytes 98308
  125.2 259.2 %copy-start.21 = (bf16[256,64]{0,1:T(8,128)(2,1)}, bf16[256,64]{0,1:T(8,128)(2,1)S(1)}, u32[]{:S(2)}) copy-start(bf16[256,64]{0,1:T(8,128)(2,1)S(1)} %fusion.62) | copy-start | bytes 98308
  125.4 257.7 %copy-start.23 = (bf16[256,64]{0,1:T(8,128)(2,1)}, bf16[256,64]{0,1:T(8,128)(2,1)S(1)}, u32[]{:S(2)}) copy-start(bf16[256,64]{0,1:T(8,128)(2,1)S(1)} %fusion.63) | copy-start | bytes 98308
  126.6 257.8 %copy-start.36 = (bf16[256,64]{0,1:T(8,128)(2,1)}, bf16[256,64]{0,1:T(8,128)(2,1)S(1)}, u32[]{:S(2)}) copy-start(bf16[256,64]{0,1:T(8,128)(2,1)S(1)} %get-tuple-element.465) | copy-start | bytes 98308
  126.6 258.4 %copy-start.34 = (bf16[256,64]{0,1:T(8,128)(2,1)}, bf16[256,64]{0,1:T(8,128)(2,1)S(1)}, u32[]{:S(2)}) copy-start(bf16[256,64]{0,1:T(8,128)(2,1)S(1)} %get-tuple-element.468) | copy-start | bytes 98308
  126.6 259.9 %copy-start.32 = (bf16[256,64]{0,1:T(8,128)(2,1)}, bf16[256,64]{0,1:T(8,128)(2,1)S(1)}, u32[]{:S(2)}) copy-start(bf16[256,64]{0,1:T(8,128)(2,1)S(1)} %get-tuple-element.471) | copy-start | bytes 98308
  126.6 261.5 %copy-start.30 = (bf16[256,64]{0,1:T(8,128)(2,1)}, bf16[256,64]{0,1:T(8,128)(2,1)S(1)}, u32[]{:S(2)}) copy-start(bf16[256,64]{0,1:T(8,128)(2,1)S(1)} %get-tuple-element.474) | copy-start | bytes 98308
  126.6 263.0 %copy-start.28 = (bf16[256,64]{0,1:T(8,128)(2,1)}, bf16[256,64]{0,1:T(8,128)(2,1)S(1)}, u32[]{:S(2)}) copy-start(bf16[256,64]{0,1:T(8,128)(2,1)S(1)} %get-tuple-element.477) | copy-start | bytes 98308
  385.0 1.0 copy-start
  386.5 1.0 copy-start.1
  388.0 1.0 copy-start.2
  389.5 1.0 copy-start.3
  391.1 1.0 copy-start.4
  394.1 1.0 copy-start.5
  403.5 46.7 %all-to-all-start = ((bf16[16,16,1024]{2,1,0:T(8,128)(2,1)}), bf16[16,16,1024]{2,1,0:T(8,128)(2,1)S(1)}, u32[]{:S(2)}, u32[]{:S(2)}) async-start(bf16[16,16,1024]{2,1,0:T(8,128)(2,1)} %bitcast.1), calls=%async_computation | async-start | bytes 1048576 | tf_op jit(solution)/shard_map/all_to_all | solution.py:143
  438.2 43.5 %copy-start.26 = (bf16[16,1024]{1,0:T(8,128)(2,1)S(1)}, bf16[16,1024]{1,0:T(8,128)(2,1)}, u32[]{:S(2)}) copy-start(bf16[16,1024]{1,0:T(8,128)(2,1)} %param.36) | copy-start | bytes 98308
  450.2 31.3 %all-to-all-start.1 = ((bf16[32,16,1024]{2,1,0:T(8,128)(2,1)}), bf16[32,16,1024]{2,1,0:T(8,128)(2,1)S(1)}, u32[]{:S(2)}, u32[]{:S(2)}) async-start(bf16[32,16,1024]{2,1,0:T(8,128)(2,1)} %bitcast.2), calls=%async_computation.1 | async-start | bytes 2097152 | tf_op jit(solution)/shard_map/all_to_all | solution.py:147
  454.4 156.5 %all-gather.5.cloned.1.call-start = ((), (), s32[]{:S(2)}) async-start(), calls=%async_computation.5 | async-start | bytes 1081344 | tf_op jit(solution)/shard_map/all_gather | solution.py:127
  454.5 158.4 %copy-start.24 = (bf16[256,64]{0,1:T(8,128)(2,1)S(1)}, bf16[256,64]{0,1:T(8,128)(2,1)}, u32[]{:S(2)}) copy-start(bf16[256,64]{0,1:T(8,128)(2,1)} %copy-done.23) | copy-start | bytes 98308
  516.5 96.5 %copy-start.22 = (bf16[256,64]{0,1:T(8,128)(2,1)S(1)}, bf16[256,64]{0,1:T(8,128)(2,1)}, u32[]{:S(2)}) copy-start(bf16[256,64]{0,1:T(8,128)(2,1)} %copy-done.21) | copy-start | bytes 98308
  516.5 96.5 %copy-start.37 = (bf16[256,64]{0,1:T(8,128)(2,1)S(1)}, bf16[256,64]{0,1:T(8,128)(2,1)}, u32[]{:S(2)}) copy-start(bf16[256,64]{0,1:T(8,128)(2,1)} %copy-done.36) | copy-start | bytes 98308
  614.3 0.8 copy-start.20
  614.3 0.8 copy-start.35
  615.6 1.0 copy-start.6
  615.6 1.0 copy-start.18
  615.6 1.0 copy-start.33
  617.1 1.0 copy-start.7
  617.1 1.0 copy-start.16
  617.1 1.0 copy-start.31
  618.7 1.0 copy-start.8
  618.7 1.0 copy-start.14
  618.7 1.0 copy-start.29
  620.2 1.0 copy-start.9
  621.7 1.0 copy-start.10
  624.8 1.0 copy-start.11
  634.1 47.2 %all-to-all-start.2 = ((bf16[16,16,1024]{2,1,0:T(8,128)(2,1)}), bf16[16,16,1024]{2,1,0:T(8,128)(2,1)S(1)}, u32[]{:S(2)}, u32[]{:S(2)}) async-start(bf16[16,16,1024]{2,1,0:T(8,128)(2,1)} %bitcast.3), calls=%async_computation.2 | async-start | bytes 1048576 | tf_op jit(solution)/shard_map/all_to_all | solution.py:143
  669.3 43.5 %copy-start.27 = (bf16[16,1024]{1,0:T(8,128)(2,1)S(1)}, bf16[16,1024]{1,0:T(8,128)(2,1)}, u32[]{:S(2)}) copy-start(bf16[16,1024]{1,0:T(8,128)(2,1)} %param.36) | copy-start | bytes 98308
  681.3 31.3 %all-to-all-start.3 = ((bf16[32,16,1024]{2,1,0:T(8,128)(2,1)}), bf16[32,16,1024]{2,1,0:T(8,128)(2,1)S(1)}, u32[]{:S(2)}, u32[]{:S(2)}) async-start(bf16[32,16,1024]{2,1,0:T(8,128)(2,1)} %bitcast.4), calls=%async_computation.3 | async-start | bytes 2097152 | tf_op jit(solution)/shard_map/all_to_all | solution.py:147
Sparse Core Ops, SparseCore 0:
  258.5 122.4 all-gather.2
  482.5 128.3 all-gather.4
where the time goes:
time: 723 us; the launch traced here: 720 us
  blocking collectives  294 us (41%)
  waiting for transfers between devices  263 us (36%)
  starting transfers between devices  72 us (10%)
  matrix products  29.4 us (4%)
  local copies, waits for them, and re-layouts  22.2 us (3%)
  between operations  20.4 us (3%)
  other arithmetic  18.3 us (3%)
    all_gather x2, waiting for transfers between devices, shards(): lax.all_gather(scaled, 'row', axis=0, tiled=True)  185 us
    unnamed x2, blocking collectives  131 us
    all_gather x1, blocking collectives, shards(): col_gathered = lax.all_gather(unit_vecs, 'row', axis=0, tiled=True)  66.2 us
    all_to_all x2, starting transfers between devices, shards(): lax.all_to_all(sent_rows, 'col', split_axis=0, concat_axis=0, tiled=True)  63.6 us
    all_gather x2, blocking collectives, shards(): row_labels = lax.all_gather(scaled, 'col', axis=0, tiled=True)  60.9 us
    all_to_all x2, waiting for transfers between devices, shards(): lax.all_to_all(sent_cols, 'row', split_axis=0, concat_axis=0, tiled=True)  54 us
    all_gather x1, blocking collectives, shards(): row_units = lax.all_gather(unit_vecs, 'col', axis=0, tiled=True)  36.6 us
    all_to_all x2, waiting for transfers between devices, shards(): lax.all_to_all(sent_rows, 'col', split_axis=0, concat_axis=0, tiled=True)  24 us
  transfers between devices with their start and end apart: 6, of which 6 were waited for; matrix products, arithmetic and copies ran while one was open for 1% of the time, Pallas kernels for 0%

commit v1 on v0

v1 whole, which is shorter than its diff:
```python
import math

import jax
import jax.numpy as jnp
from jax import lax
from jax.experimental import pallas as pl
from jax.experimental.pallas import tpu as pltpu
from jax.sharding import PartitionSpec as P

MIXING = 0.9
SHARPNESS = 3.0
EPSILON = 1e-06

SIDE = 8
CHUNK = 128
PIECE = 16
LANES = 128
MESH = pl.DeviceIdType.MESH
FAR_FIRST = (4, 3, 5, 2, 6, 1, 7)
NEAR_FIRST = (1, 7, 2, 6, 3, 5, 4)

UNIT_SWAP, LABEL_SWAP, UNIT_GATHER, UNIT_PASS, LABEL_GATHER, DEGREE, REDUCE1, GATHER2, REDUCE2, FINAL = range(10)
PHASES = 10


def spread_kernel(
    mask_ref,
    emb_ref,
    lab_ref,
    out_ref,
    uj,
    ui,
    kmat,
    lab,
    sc1,
    sc2,
    part1,
    part2,
    rcv1,
    rcv2,
    deg,
    fin,
    outb,
    send_sem,
    recv_sem,
):
    row = lax.axis_index("row")
    col = lax.axis_index("col")
    y = lax.div(row, 4)
    z_lo = lax.rem(row, 4)
    z_hi = lax.div(col, 8)
    c = lax.rem(col, 8)
    core = lax.rem(col, 2)
    z = z_hi * 4 + z_lo

    def at(new_y, new_z):
        return (new_y * 4 + lax.rem(new_z, 4), lax.div(new_z, 4) * 8 + c)

    def gather_peer(k):
        return at(lax.rem(y + core * k, SIDE), lax.rem(z + (1 - core) * k, SIDE))

    def reduce_peer(k):
        return at(lax.rem(y + (1 - core) * k, SIDE), lax.rem(z + core * k, SIDE))

    def swap_index(k):
        return lax.rem(c + k, SIDE)

    def swap_peer(k):
        return (row, z_hi * 8 + swap_index(k))

    partner = (row, z_hi * 8 + (c + 1 - 2 * core))

    barrier = pltpu.get_barrier_semaphore()
    for k in range(1, SIDE):
        for peer in (gather_peer(k), reduce_peer(k), swap_peer(k)):
            pl.semaphore_signal(barrier, inc=1, device_id=peer, device_id_type=MESH)

    started = []

    def send(phase, k, src, dst, device):
        copy = pltpu.make_async_remote_copy(
            src_ref=src,
            dst_ref=dst,
            send_sem=send_sem.at[phase, k],
            recv_sem=recv_sem.at[phase, k],
            device_id=device,
            device_id_type=MESH,
        )
        copy.start()
        started.append(copy)
        return copy

    own_rows = pl.ds(pl.multiple_of(c * PIECE, PIECE), PIECE)
    own_lanes = pl.ds(pl.multiple_of(c * LANES, LANES), LANES)
    values = emb_ref[...].astype(jnp.float32)
    norm = lax.rsqrt(jnp.sum(values * values, axis=1, keepdims=True) + EPSILON)
    uj[0, own_rows, :] = (values * norm).astype(jnp.bfloat16)
    lab[0, own_rows, :] = lab_ref[:, own_lanes]

    pl.semaphore_wait(barrier, 3 * (SIDE - 1))

    unit_swaps = [
        send(UNIT_SWAP, k, uj.at[0, own_rows, :], uj.at[0, own_rows, :], swap_peer(k)) for k in range(1, SIDE)
    ]
    label_swaps = []
    for k in range(1, SIDE):
        lanes = pl.ds(pl.multiple_of(swap_index(k) * LANES, LANES), LANES)
        label_swaps.append(
            send(LABEL_SWAP, k, lab_ref.at[:, lanes], lab.at[0, own_rows, :], swap_peer(k))
        )

    for copy in unit_swaps:
        copy.wait_recv()
    unit_gathers = {
        k: send(UNIT_GATHER, k, uj.at[0], uj.at[k], gather_peer(k)) for k in FAR_FIRST
    }
    for copy in label_swaps:
        copy.wait_recv()
    label_gathers = [
        send(LABEL_GATHER, k, lab.at[0], lab.at[k], gather_peer(k)) for k in FAR_FIRST
    ]
    ui[0] = uj[0]
    unit_passes = []
    for k in NEAR_FIRST:
        unit_gathers[k].wait_recv()
        unit_passes.append(send(UNIT_PASS, k, uj.at[k], ui.at[k], partner))
    for copy in unit_passes:
        copy.wait_recv()

    scale = SHARPNESS * math.sqrt(emb_ref.shape[1]) * math.log2(math.e)
    lane = lax.broadcasted_iota(jnp.int32, (1, 2 * CHUNK), 1)

    def block_of(chunk_y, chunk_z):
        return chunk_y * 4 + lax.rem(chunk_z, 4)

    def back(position, k):
        return lax.rem(position + SIDE - k, SIDE)

    def kept(row_block, col_block):
        low = jnp.minimum(row_block, col_block)
        high = jnp.maximum(row_block, col_block)
        return jnp.where(row_block == col_block, 1, mask_ref[low, high]).astype(jnp.float32)

    def make_columns(group, carry):
        columns = uj[pl.ds(2 * group, 2)].reshape(2 * CHUNK, emb_ref.shape[1])
        col_blocks = [
            block_of(back(y, core * (2 * group + half)), back(z, (1 - core) * (2 * group + half)))
            for half in range(2)
        ]
        sums = jnp.zeros((1, 2 * CHUNK), jnp.float32)
        for k in range(SIDE):
            row_block = block_of(back(y, (1 - core) * k), back(z, core * k))
            cosine = lax.dot_general(
                ui[k], columns, (((1,), (1,)), ((), ())), preferred_element_type=jnp.float32
            )
            keep = jnp.where(
                lane < CHUNK, kept(row_block, col_blocks[0]), kept(row_block, col_blocks[1])
            )
            weights = jnp.exp2(cosine * scale) * keep
            if k == 0:
                own_row = lax.broadcasted_iota(jnp.int32, weights.shape, 0)
                own_col = lax.broadcasted_iota(jnp.int32, weights.shape, 1) + group * (2 * CHUNK)
                weights = jnp.where(own_row == own_col, 0.0, weights)
            weights = weights.astype(jnp.bfloat16)
            kmat[group, k * CHUNK : (k + 1) * CHUNK, :] = weights
            sums = sums + jnp.sum(weights.astype(jnp.float32), axis=0, keepdims=True)
        deg[0, pl.ds(2 * group, 1), :] = sums[:, :CHUNK]
        deg[0, pl.ds(2 * group + 1, 1), :] = sums[:, CHUNK:]
        return carry

    lax.fori_loop(0, SIDE // 2, make_columns, 0)

    degrees = [send(DEGREE, k, deg.at[0], deg.at[k], gather_peer(k)) for k in FAR_FIRST]
    for copy in label_gathers:
        copy.wait_recv()
    for copy in degrees:
        copy.wait_recv()
    degree = deg[0]
    for k in range(1, SIDE):
        degree = degree + pltpu.roll(deg[k], k, 0)
    inv_root = jnp.transpose(lax.rsqrt(degree))
    for k in range(SIDE):
        sc1[k] = (lab[k].astype(jnp.float32) * inv_root[:, k : k + 1]).astype(jnp.bfloat16)
    own_root = inv_root[:, 0:1]
    seeds = lab[0].astype(jnp.float32)

    def spread_rows(scaled, k):
        total = jnp.zeros((CHUNK, LANES), jnp.float32)
        for group in range(SIDE // 2):
            total = total + jnp.dot(
                kmat[group, k * CHUNK : (k + 1) * CHUNK, :],
                scaled[2 * group : 2 * group + 2].reshape(2 * CHUNK, LANES),
                preferred_element_type=jnp.float32,
            )
        return total

    def iterate(phase, scaled, part, rcv):
        copies = []
        for k in FAR_FIRST:
            part[k] = spread_rows(scaled, k).astype(jnp.bfloat16)
            copies.append(send(phase, k, part.at[k], rcv.at[k], reduce_peer(SIDE - k)))
        spread = spread_rows(scaled, 0)
        for copy in copies:
            copy.wait_recv()
        for k in range(1, SIDE):
            spread = spread + rcv[k].astype(jnp.float32)
        return MIXING * own_root * spread + (1.0 - MIXING) * seeds

    current = iterate(REDUCE1, sc1, part1, rcv1)
    sc2[0] = (own_root * current).astype(jnp.bfloat16)
    gathers = [send(GATHER2, k, sc2.at[0], sc2.at[k], gather_peer(k)) for k in FAR_FIRST]
    for copy in gathers:
        copy.wait_recv()
    current = iterate(REDUCE2, sc2, part2, rcv2)
    fin[...] = current.astype(jnp.bfloat16)
    outb[:, own_lanes] = fin[own_rows, :]
    finals = []
    for k in range(1, SIDE):
        rows = pl.ds(pl.multiple_of(swap_index(k) * PIECE, PIECE), PIECE)
        finals.append(send(FINAL, k, fin.at[rows, :], outb.at[:, own_lanes], swap_peer(k)))
    for copy in finals:
        copy.wait_recv()
    out_ref[...] = outb[...]
    for copy in started:
        copy.wait_send()


def shards(embeddings, labels, tile_mask):
    width = embeddings.shape[1]
    vmem = pl.BlockSpec(memory_space=pltpu.VMEM)
    chunks = (SIDE, CHUNK, LANES)
    return pl.pallas_call(
        spread_kernel,
        out_shape=jax.ShapeDtypeStruct(labels.shape, jnp.bfloat16),
        in_specs=[pl.BlockSpec(memory_space=pltpu.SMEM), vmem, vmem],
        out_specs=vmem,
        scratch_shapes=[
            pltpu.VMEM((SIDE, CHUNK, width), jnp.bfloat16),
            pltpu.VMEM((SIDE, CHUNK, width), jnp.bfloat16),
            pltpu.VMEM((SIDE // 2, SIDE * CHUNK, 2 * CHUNK), jnp.bfloat16),
            pltpu.VMEM(chunks, jnp.bfloat16),
            pltpu.VMEM(chunks, jnp.bfloat16),
            pltpu.VMEM(chunks, jnp.bfloat16),
            pltpu.VMEM(chunks, jnp.bfloat16),
            pltpu.VMEM(chunks, jnp.bfloat16),
            pltpu.VMEM(chunks, jnp.bfloat16),
            pltpu.VMEM(chunks, jnp.bfloat16),
            pltpu.VMEM((SIDE, SIDE, CHUNK), jnp.float32),
            pltpu.VMEM((CHUNK, LANES), jnp.bfloat16),
            pltpu.VMEM(labels.shape, jnp.bfloat16),
            pltpu.SemaphoreType.DMA((PHASES, SIDE)),
            pltpu.SemaphoreType.DMA((PHASES, SIDE)),
        ],
        compiler_params=pltpu.CompilerParams(collective_id=0, has_side_effects=True),
    )(tile_mask, embeddings, labels)


def solution(mesh):
    placed = (P(("row", "col"), None), P(("row", "col"), None), P())
    return jax.shard_map(
        shards, mesh=mesh, in_specs=placed, out_specs=P(("row", "col"), None), check_vma=False
    )
```

time: 723 us -> 62.4 us (0.09)
  blocking collectives: 294 us -> 0 us
  waiting for transfers between devices: 263 us -> 0 us
  starting transfers between devices: 72 us -> 0 us
  Pallas kernels: 0 us -> 60.7 us
  matrix products: 29.4 us -> 0 us
  local copies, waits for them, and re-layouts: 22.2 us -> 1.38 us
  between operations: 20.4 us -> 0.01 us
  other arithmetic: 18.3 us -> 0 us
    all_gather x2 -> x0, waiting for transfers between devices: 185 us -> none  [shards(): lax.all_gather(scaled, 'row', axis=0, tiled=True)]
    all_gather x4 -> x0, blocking collectives: 164 us -> none  [the longest x1 66.2 us: shards(): col_gathered = lax.all_gather(unit_vecs, 'row', axis=0, tiled=True)]
    unnamed x2 -> x0, blocking collectives: 131 us -> none
    all_to_all x4 -> x0, waiting for transfers between devices: 78 us -> none  [the longest x2 54 us: shards(): lax.all_to_all(sent_cols, 'row', split_axis=0, concat_axis=0, tiled=True)]
    all_to_all x4 -> x0, starting transfers between devices: 72 us -> none  [the longest x2 63.6 us: shards(): lax.all_to_all(sent_rows, 'col', split_axis=0, concat_axis=0, tiled=True)]
    pallas_call x0 -> x1, Pallas kernels: none -> 60.7 us  [shards(): pl.pallas_call(spread_kernel, out_shape=jax.ShapeDtypeStruct(labels.shape...]
    dot_general x49 -> x0, matrix products: 29.4 us -> none  [the longest x16 10.1 us: both_terms(): jnp.dot(row_kernel, part_labels, preferred_element_type=jnp.float32)]
    unnamed x109 -> x1, local copies, waits for them, and re-layouts: 18 us -> 1.38 us
  transfers between devices with their start and end apart: 6 -> 0, of which waited for: 6 -> 0; matrix products, arithmetic and copies ran while one was open for 1% -> 0% of each run, Pallas kernels for 0% -> 0%
where the time goes in v1:
time: 62.4 us; the launch traced here: 62.1 us
  Pallas kernels  60.7 us (97%)
  local copies, waits for them, and re-layouts  1.38 us (2%)
    pallas_call x1, Pallas kernels, shards(): pl.pallas_call(spread_kernel, out_shape=jax.ShapeDtypeStruct(labels.shape...  60.7 us
    unnamed x1, local copies, waits for them, and re-layouts  1.38 us

profile of v1, /device:TPU:1, one launch (start us, length us, event | category | flops | bytes accessed | tf_op | source)
XLA Modules:
  0.0 62.1 jit_solution(4128002383935601553)
XLA Ops:
  0.0 60.7 %shard_map.37 = bf16[16,1024]{1,0:T(8,128)(2,1)} custom-call(s32[32,32]{1,0:T(8,128)} %mask_ref.1, bf16[16,256]{1,0:T(8,128)(2,1)} %emb_ref.1, bf16[16,1024]{1,0:T(8,128)(2,1)} %lab_ref.1), custom_call_target="tpu_custom_call" | custom-call | tf_op jit(solution)/shard_map/pallas_call | solution.py:232
  60.7 1.4 %copy.5 = bf16[16,1024]{1,0:T(8,128)(2,1)} copy(bf16[16,1024]{1,0:T(8,128)(2,1)} %shard_map.37) | data formatting | bytes 65536

commit v2 on v1

v2 whole, which is shorter than its diff:
```python
import math

import jax
import jax.numpy as jnp
from jax import lax
from jax.experimental import pallas as pl
from jax.experimental.pallas import tpu as pltpu
from jax.sharding import PartitionSpec as P

MIXING = 0.9
SHARPNESS = 3.0
EPSILON = 1e-06

SIDE = 8
CHUNK = 128
PIECE = 16
LANES = 128
MESH = pl.DeviceIdType.MESH
FAR_FIRST = (4, 3, 5, 2, 6, 1, 7)
NEAR_FIRST = (1, 7, 2, 6, 3, 5, 4)

HALF = CHUNK // 2
UNIT_SWAP, LABEL_SWAP, UNIT_GATHER, UNIT_PASS, LABEL_GATHER, DEGREE = range(6)
REDUCE1, GATHER2, REDUCE2 = (6, 7), (8, 9), (10, 11)
FINAL = 12
PHASES = 13
LOAD_UNITS, LOAD_LABELS, LOAD_MASK, STORE_OWN = range(4)


def spread_kernel(
    mask_hbm,
    emb_hbm,
    lab_hbm,
    out_hbm,
    mask_ref,
    emb_ref,
    uj,
    ui,
    kmat,
    lab,
    sc1,
    sc2,
    part1,
    part2,
    rcv1,
    rcv2,
    deg,
    fin,
    send_sem,
    recv_sem,
    local_sem,
):
    row = lax.axis_index("row")
    col = lax.axis_index("col")
    y = lax.div(row, 4)
    z_lo = lax.rem(row, 4)
    z_hi = lax.div(col, 8)
    c = lax.rem(col, 8)
    core = lax.rem(col, 2)
    z = z_hi * 4 + z_lo

    def at(new_y, new_z):
        return (new_y * 4 + lax.rem(new_z, 4), lax.div(new_z, 4) * 8 + c)

    def gather_peer(k):
        return at(lax.rem(y + core * k, SIDE), lax.rem(z + (1 - core) * k, SIDE))

    def reduce_peer(k):
        return at(lax.rem(y + (1 - core) * k, SIDE), lax.rem(z + core * k, SIDE))

    def swap_index(k):
        return lax.rem(c + k, SIDE)

    def swap_peer(k):
        return (row, z_hi * 8 + swap_index(k))

    partner = (row, z_hi * 8 + (c + 1 - 2 * core))

    own_rows = pl.ds(pl.multiple_of(c * PIECE, PIECE), PIECE)
    own_lanes = pl.ds(pl.multiple_of(c * LANES, LANES), LANES)

    def local(slot, src, dst):
        copy = pltpu.make_async_copy(src, dst, local_sem.at[slot])
        copy.start()
        return copy

    load_units = local(LOAD_UNITS, emb_hbm, emb_ref)
    load_labels = local(LOAD_LABELS, lab_hbm.at[:, own_lanes], lab.at[0, own_rows, :])
    load_mask = local(LOAD_MASK, mask_hbm, mask_ref)
    barrier = pltpu.get_barrier_semaphore()
    for k in range(1, SIDE):
        for peer in (gather_peer(k), reduce_peer(k), swap_peer(k)):
            pl.semaphore_signal(barrier, inc=1, device_id=peer, device_id_type=MESH)

    def describe(phase, src, dst, device, slot=None):
        return pltpu.make_async_remote_copy(
            src_ref=src,
            dst_ref=dst,
            send_sem=send_sem.at[phase],
            recv_sem=recv_sem.at[phase if slot is None else PHASES + slot],
            device_id=device,
            device_id_type=MESH,
        )

    def send(phase, src, dst, device, slot=None):
        copy = describe(phase, src, dst, device, slot)
        copy.start()
        return copy

    sent = []

    def whole(phase, ref):
        copy = describe(phase, ref, ref, partner)
        sent.append(copy)
        return copy

    load_units.wait()
    values = emb_ref[...].astype(jnp.float32)
    norm = lax.rsqrt(jnp.sum(values * values, axis=1, keepdims=True) + EPSILON)
    uj[0, own_rows, :] = (values * norm).astype(jnp.bfloat16)

    pl.semaphore_wait(barrier, 3 * (SIDE - 1))

    for k in range(1, SIDE):
        send(UNIT_SWAP, uj.at[0, own_rows, :], uj.at[0, own_rows, :], swap_peer(k))
    for k in range(1, SIDE):
        lanes = pl.ds(pl.multiple_of(swap_index(k) * LANES, LANES), LANES)
        send(LABEL_SWAP, lab_hbm.at[:, lanes], lab.at[0, own_rows, :], swap_peer(k))

    others = slice(1, SIDE)
    whole(UNIT_SWAP, uj.at[0, 0 : (SIDE - 1) * PIECE, :]).wait_recv()
    unit_gathers = {
        k: send(UNIT_GATHER, uj.at[0], uj.at[k], gather_peer(k), slot=k - 1) for k in FAR_FIRST
    }
    whole(UNIT_GATHER, uj.at[others])
    load_labels.wait()
    whole(LABEL_SWAP, lab.at[0, 0 : (SIDE - 1) * PIECE, :]).wait_recv()
    for k in FAR_FIRST:
        send(LABEL_GATHER, lab.at[0], lab.at[k], gather_peer(k))
    ui[0] = uj[0]
    for k in NEAR_FIRST:
        unit_gathers[k].wait_recv()
        send(UNIT_PASS, uj.at[k], ui.at[k], partner)
    whole(UNIT_PASS, ui.at[others]).wait_recv()
    load_mask.wait()

    scale = SHARPNESS * math.sqrt(emb_ref.shape[1]) * math.log2(math.e)
    lane = lax.broadcasted_iota(jnp.int32, (1, 2 * CHUNK), 1)

    def block_of(chunk_y, chunk_z):
        return chunk_y * 4 + lax.rem(chunk_z, 4)

    def back(position, k):
        return lax.rem(position + SIDE - k, SIDE)

    def kept(row_block, col_block):
        low = jnp.minimum(row_block, col_block)
        high = jnp.maximum(row_block, col_block)
        return jnp.where(row_block == col_block, 1, mask_ref[low, high]).astype(jnp.float32)

    def make_columns(group, carry):
        columns = uj[pl.ds(2 * group, 2)].reshape(2 * CHUNK, emb_ref.shape[1])
        col_blocks = [
            block_of(back(y, core * (2 * group + half)), back(z, (1 - core) * (2 * group + half)))
            for half in range(2)
        ]
        sums = jnp.zeros((1, 2 * CHUNK), jnp.float32)
        for k in range(SIDE):
            row_block = block_of(back(y, (1 - core) * k), back(z, core * k))
            cosine = lax.dot_general(
                ui[k], columns, (((1,), (1,)), ((), ())), preferred_element_type=jnp.float32
            )
            keep = jnp.where(
                lane < CHUNK, kept(row_block, col_blocks[0]), kept(row_block, col_blocks[1])
            )
            weights = jnp.exp2(cosine * scale) * keep
            if k == 0:
                own_row = lax.broadcasted_iota(jnp.int32, weights.shape, 0)
                own_col = lax.broadcasted_iota(jnp.int32, weights.shape, 1) + group * (2 * CHUNK)
                weights = jnp.where(own_row == own_col, 0.0, weights)
            weights = weights.astype(jnp.bfloat16)
            kmat[k, :, pl.ds(pl.multiple_of(group * 2 * CHUNK, 2 * CHUNK), 2 * CHUNK)] = weights
            sums = sums + jnp.sum(weights.astype(jnp.float32), axis=0, keepdims=True)
        deg[0, pl.ds(2 * group, 1), :] = sums[:, :CHUNK]
        deg[0, pl.ds(2 * group + 1, 1), :] = sums[:, CHUNK:]
        return carry

    lax.fori_loop(0, SIDE // 2, make_columns, 0)

    for k in FAR_FIRST:
        send(DEGREE, deg.at[0], deg.at[k], gather_peer(k))
    whole(LABEL_GATHER, lab.at[others]).wait_recv()
    whole(DEGREE, deg.at[others]).wait_recv()
    degree = deg[0]
    for k in range(1, SIDE):
        degree = degree + pltpu.roll(deg[k], k, 0)
    inv_root = jnp.transpose(lax.rsqrt(degree))
    for k in range(SIDE):
        sc1[k] = (lab[k].astype(jnp.float32) * inv_root[:, k : k + 1]).astype(jnp.bfloat16)
    own_root = inv_root[:, 0:1]
    seeds = lab[0].astype(jnp.float32)

    def rows_of(half):
        return pl.ds(half * HALF, HALF)

    def iterate(phases, scaled, part, rcv, finish):
        spreads = []
        for half in range(2):
            rows = rows_of(half)
            spread = jnp.dot(
                kmat[:, rows, :].reshape(SIDE * HALF, SIDE * CHUNK),
                scaled[...].reshape(SIDE * CHUNK, LANES),
                preferred_element_type=jnp.float32,
            ).reshape(SIDE, HALF, LANES)
            spreads.append(spread[0])
            for k in FAR_FIRST:
                part[k, rows, :] = spread[k].astype(jnp.bfloat16)
            for k in FAR_FIRST:
                send(phases[half], part.at[k, rows, :], rcv.at[k, rows, :], reduce_peer(SIDE - k))
        for half in range(2):
            whole(phases[half], rcv.at[others, rows_of(half), :]).wait_recv()
            total = spreads[half]
            for k in range(1, SIDE):
                total = total + rcv[k, rows_of(half), :].astype(jnp.float32)
            rows = slice(half * HALF, (half + 1) * HALF)
            finish(half, MIXING * own_root[rows] * total + (1.0 - MIXING) * seeds[rows])

    def finish_first(half, current):
        rows = rows_of(half)
        root = own_root[half * HALF : (half + 1) * HALF]
        sc2[0, rows, :] = (root * current).astype(jnp.bfloat16)
        for k in FAR_FIRST:
            send(GATHER2[half], sc2.at[0, rows, :], sc2.at[k, rows, :], gather_peer(k))

    def finish_last(half, current):
        fin[rows_of(half), :] = current.astype(jnp.bfloat16)

    iterate(REDUCE1, sc1, part1, rcv1, finish_first)
    for half in range(2):
        whole(GATHER2[half], sc2.at[others, rows_of(half), :]).wait_recv()
    iterate(REDUCE2, sc2, part2, rcv2, finish_last)
    store_own = local(STORE_OWN, fin.at[own_rows, :], out_hbm.at[:, own_lanes])
    for k in range(1, SIDE):
        rows = pl.ds(pl.multiple_of(swap_index(k) * PIECE, PIECE), PIECE)
        send(FINAL, fin.at[rows, :], out_hbm.at[:, own_lanes], swap_peer(k))
    whole(FINAL, fin.at[0 : (SIDE - 1) * PIECE, :]).wait_recv()
    store_own.wait()
    for copy in sent:
        copy.wait_send()


def shards(embeddings, labels, tile_mask):
    width = embeddings.shape[1]
    anywhere = pl.BlockSpec(memory_space=pl.ANY)
    units = pltpu.VMEM((SIDE, CHUNK, width), jnp.bfloat16)
    chunks = pltpu.VMEM((SIDE, CHUNK, LANES), jnp.bfloat16)
    return pl.pallas_call(
        spread_kernel,
        out_shape=jax.ShapeDtypeStruct(labels.shape, jnp.bfloat16),
        in_specs=[anywhere] * 3,
        out_specs=anywhere,
        scratch_shapes=[
            pltpu.SMEM(tile_mask.shape, jnp.int32),
            pltpu.VMEM(embeddings.shape, jnp.bfloat16),
            units,
            units,
            pltpu.VMEM((SIDE, CHUNK, SIDE * CHUNK), jnp.bfloat16),
            chunks,
            chunks,
            chunks,
            chunks,
            chunks,
            chunks,
            chunks,
            pltpu.VMEM((SIDE, SIDE, CHUNK), jnp.float32),
            pltpu.VMEM((CHUNK, LANES), jnp.bfloat16),
            pltpu.SemaphoreType.DMA((PHASES,)),
            pltpu.SemaphoreType.DMA((PHASES + SIDE - 1,)),
            pltpu.SemaphoreType.DMA((4,)),
        ],
        compiler_params=pltpu.CompilerParams(collective_id=0, has_side_effects=True),
    )(tile_mask, embeddings, labels)


def solution(mesh):
    placed = (P(("row", "col"), None), P(("row", "col"), None), P())
    return jax.shard_map(
        shards, mesh=mesh, in_specs=placed, out_specs=P(("row", "col"), None), check_vma=False
    )
```

time: 62.4 us -> 59.6 us (0.955)
  Pallas kernels: 60.7 us -> 58 us
    pallas_call x1, Pallas kernels: 60.7 us -> 58 us  [shards(): pl.pallas_call(spread_kernel, out_shape=jax.ShapeDtypeStruct(labels.shape...]
where the time goes in v2:
time: 59.6 us; the launch traced here: 59.4 us
  Pallas kernels  58 us (97%)
  local copies, waits for them, and re-layouts  1.38 us (2%)
    pallas_call x1, Pallas kernels, shards(): pl.pallas_call(spread_kernel, out_shape=jax.ShapeDtypeStruct(labels.shape...  58 us
    unnamed x1, local copies, waits for them, and re-layouts  1.38 us

profile of v2, /device:TPU:1, one launch (start us, length us, event | category | flops | bytes accessed | tf_op | source)
XLA Modules:
  0.0 59.4 jit_solution(12828644488466932309)
XLA Ops:
  0.0 58.0 %shard_map.37 = bf16[16,1024]{1,0:T(8,128)(2,1)} custom-call(s32[32,32]{1,0:T(8,128)} %mask_hbm.1, bf16[16,256]{1,0:T(8,128)(2,1)} %emb_hbm.1, bf16[16,1024]{1,0:T(8,128)(2,1)} %lab_hbm.1), custom_call_target="tpu_custom_call" | custom-call | tf_op jit(solution)/shard_map/pallas_call | solution.py:257
  58.0 1.4 %copy.5 = bf16[16,1024]{1,0:T(8,128)(2,1)} copy(bf16[16,1024]{1,0:T(8,128)(2,1)} %shard_map.37) | data formatting | bytes 65536

commit v3 on v2

--- a/solution.py
+++ b/solution.py
@@ -22,8 +22,9 @@
 HALF = CHUNK // 2
 UNIT_SWAP, LABEL_SWAP, UNIT_GATHER, UNIT_PASS, LABEL_GATHER, DEGREE = range(6)
 REDUCE1, GATHER2, REDUCE2 = (6, 7), (8, 9), (10, 11)
-FINAL = 12
-PHASES = 13
+FINAL, PIECE_GATHER, CROSS = 12, 13, 14
+PHASES = 15
+SLOTS = SIDE - 1 + 3
 LOAD_UNITS, LOAD_LABELS, LOAD_MASK, STORE_OWN = range(4)
 
 
@@ -74,7 +75,17 @@
     def swap_peer(k):
         return (row, z_hi * 8 + swap_index(k))
 
-    partner = (row, z_hi * 8 + (c + 1 - 2 * core))
+    partner_c = c + 1 - 2 * core
+    partner = (row, z_hi * 8 + partner_c)
+
+    def beside(position):
+        return (position[0], lax.div(position[1], 8) * 8 + partner_c)
+
+    def cross_peer(k):
+        return beside(reduce_peer(k))
+
+    def x_peer(k):
+        return swap_peer(2 * k)
 
     own_rows = pl.ds(pl.multiple_of(c * PIECE, PIECE), PIECE)
     own_lanes = pl.ds(pl.multiple_of(c * LANES, LANES), LANES)
@@ -89,7 +100,7 @@
     load_mask = local(LOAD_MASK, mask_hbm, mask_ref)
     barrier = pltpu.get_barrier_semaphore()
     for k in range(1, SIDE):
-        for peer in (gather_peer(k), reduce_peer(k), swap_peer(k)):
+        for peer in (gather_peer(k), reduce_peer(k), swap_peer(k), beside(gather_peer(k))):
             pl.semaphore_signal(barrier, inc=1, device_id=peer, device_id_type=MESH)
 
     def describe(phase, src, dst, device, slot=None):
@@ -114,33 +125,57 @@
         sent.append(copy)
         return copy
 
+    low, high = slice(0, LANES), slice(LANES, 2 * LANES)
     load_units.wait()
     values = emb_ref[...].astype(jnp.float32)
     norm = lax.rsqrt(jnp.sum(values * values, axis=1, keepdims=True) + EPSILON)
     uj[0, own_rows, :] = (values * norm).astype(jnp.bfloat16)
 
-    pl.semaphore_wait(barrier, 3 * (SIDE - 1))
-
-    for k in range(1, SIDE):
-        send(UNIT_SWAP, uj.at[0, own_rows, :], uj.at[0, own_rows, :], swap_peer(k))
+    pl.semaphore_wait(barrier, 4 * (SIDE - 1))
+
+    for k in range(1, SIDE):
+        send(UNIT_SWAP, uj.at[0, own_rows, low], uj.at[0, own_rows, low], swap_peer(k))
+    piece = uj.at[0, own_rows, high]
+    for k in FAR_FIRST:
+        send(PIECE_GATHER, piece, uj.at[k, own_rows, high], gather_peer(k))
+        send(PIECE_GATHER, piece, uj.at[k, own_rows, high], cross_peer(k))
+    send(PIECE_GATHER, piece, piece, partner)
     for k in range(1, SIDE):
         lanes = pl.ds(pl.multiple_of(swap_index(k) * LANES, LANES), LANES)
         send(LABEL_SWAP, lab_hbm.at[:, lanes], lab.at[0, own_rows, :], swap_peer(k))
 
     others = slice(1, SIDE)
-    whole(UNIT_SWAP, uj.at[0, 0 : (SIDE - 1) * PIECE, :]).wait_recv()
+    whole(UNIT_SWAP, uj.at[0, 0 : (SIDE - 1) * PIECE, low]).wait_recv()
     unit_gathers = {
-        k: send(UNIT_GATHER, uj.at[0], uj.at[k], gather_peer(k), slot=k - 1) for k in FAR_FIRST
+        k: send(UNIT_GATHER, uj.at[0, :, low], uj.at[k, :, low], gather_peer(k), slot=k - 1)
+        for k in FAR_FIRST
     }
-    whole(UNIT_GATHER, uj.at[others])
+    whole(UNIT_GATHER, uj.at[others, :, low])
+    whole(PIECE_GATHER, uj.at[0:5, 0 : 3 * PIECE, low]).wait_recv()
+    pair = lax.div(c, 2) * 2 * PIECE
+
+    def pair_rows(start):
+        return pl.ds(pl.multiple_of(start, 2 * PIECE), 2 * PIECE)
+
+    block = uj.at[:, pair_rows(pair), high]
+    crosses = {k: send(CROSS, block, block, x_peer(k), slot=SIDE - 2 + k) for k in (2, 1, 3)}
+    whole(CROSS, uj.at[:, 0 : 6 * PIECE, high])
+
+    def pass_pair(start):
+        send(UNIT_PASS, uj.at[others, pair_rows(start), high], ui.at[others, pair_rows(start), high], partner)
+
+    pass_pair(pair)
     load_labels.wait()
     whole(LABEL_SWAP, lab.at[0, 0 : (SIDE - 1) * PIECE, :]).wait_recv()
     for k in FAR_FIRST:
         send(LABEL_GATHER, lab.at[0], lab.at[k], gather_peer(k))
-    ui[0] = uj[0]
     for k in NEAR_FIRST:
         unit_gathers[k].wait_recv()
-        send(UNIT_PASS, uj.at[k], ui.at[k], partner)
+        send(UNIT_PASS, uj.at[k, :, low], ui.at[k, :, low], partner)
+    for k in (1, 3, 2):
+        crosses[k].wait_recv()
+        pass_pair(lax.rem(pair + (4 - k) * 2 * PIECE, CHUNK))
+    ui[0] = uj[0]
     whole(UNIT_PASS, ui.at[others]).wait_recv()
     load_mask.wait()
 
@@ -275,7 +310,7 @@
             pltpu.VMEM((SIDE, SIDE, CHUNK), jnp.float32),
             pltpu.VMEM((CHUNK, LANES), jnp.bfloat16),
             pltpu.SemaphoreType.DMA((PHASES,)),
-            pltpu.SemaphoreType.DMA((PHASES + SIDE - 1,)),
+            pltpu.SemaphoreType.DMA((PHASES + SLOTS,)),
             pltpu.SemaphoreType.DMA((4,)),
         ],
         compiler_params=pltpu.CompilerParams(collective_id=0, has_side_effects=True),

time: 59.6 us -> 57.2 us (0.960)
  Pallas kernels: 58 us -> 55.6 us
    pallas_call x1, Pallas kernels: 58 us -> 55.6 us  [shards(): pl.pallas_call(spread_kernel, out_shape=jax.ShapeDtypeStruct(labels.shape...]
where the time goes in v3:
time: 57.2 us; the launch traced here: 57 us
  Pallas kernels  55.6 us (97%)
  local copies, waits for them, and re-layouts  1.38 us (2%)
    pallas_call x1, Pallas kernels, shards(): pl.pallas_call(spread_kernel, out_shape=jax.ShapeDtypeStruct(labels.shape...  55.6 us
    unnamed x1, local copies, waits for them, and re-layouts  1.38 us

profile of v3, /device:TPU:1, one launch (start us, length us, event | category | flops | bytes accessed | tf_op | source)
XLA Modules:
  0.0 57.0 jit_solution(7850959955248812218)
XLA Ops:
  0.0 55.6 %shard_map.37 = bf16[16,1024]{1,0:T(8,128)(2,1)} custom-call(s32[32,32]{1,0:T(8,128)} %mask_hbm.1, bf16[16,256]{1,0:T(8,128)(2,1)} %emb_hbm.1, bf16[16,1024]{1,0:T(8,128)(2,1)} %lab_hbm.1), custom_call_target="tpu_custom_call" | custom-call | tf_op jit(solution)/shard_map/pallas_call | solution.py:292
  55.6 1.4 %copy.5 = bf16[16,1024]{1,0:T(8,128)(2,1)} copy(bf16[16,1024]{1,0:T(8,128)(2,1)} %shard_map.37) | data formatting | bytes 65536

commit v4 on v3

--- a/solution.py
+++ b/solution.py
@@ -21,18 +21,19 @@
 
 HALF = CHUNK // 2
 UNIT_SWAP, LABEL_SWAP, UNIT_GATHER, UNIT_PASS, LABEL_GATHER, DEGREE = range(6)
-REDUCE1, GATHER2, REDUCE2 = (6, 7), (8, 9), (10, 11)
-FINAL, PIECE_GATHER, CROSS = 12, 13, 14
-PHASES = 15
+REDUCE1, GATHER2 = (6, 7), (8, 9)
+REDUCE2, OWN_REDUCE2, PIECE_GATHER, CROSS = 10, 11, 12, 13
+PHASES = 14
 SLOTS = SIDE - 1 + 3
-LOAD_UNITS, LOAD_LABELS, LOAD_MASK, STORE_OWN = range(4)
+LOAD_UNITS, LOAD_LABELS, LOAD_MASK, STORE_ROOT, STORE_OWN = range(5)
 
 
 def spread_kernel(
     mask_hbm,
     emb_hbm,
     lab_hbm,
-    out_hbm,
+    parts_hbm,
+    root_hbm,
     mask_ref,
     emb_ref,
     uj,
@@ -44,9 +45,9 @@
     part1,
     part2,
     rcv1,
-    rcv2,
     deg,
-    fin,
+    root,
+    root_wide,
     send_sem,
     recv_sem,
     local_sem,
@@ -175,10 +176,6 @@
     for k in (1, 3, 2):
         crosses[k].wait_recv()
         pass_pair(lax.rem(pair + (4 - k) * 2 * PIECE, CHUNK))
-    ui[0] = uj[0]
-    whole(UNIT_PASS, ui.at[others]).wait_recv()
-    load_mask.wait()
-
     scale = SHARPNESS * math.sqrt(emb_ref.shape[1]) * math.log2(math.e)
     lane = lax.broadcasted_iota(jnp.int32, (1, 2 * CHUNK), 1)
 
@@ -193,35 +190,40 @@
         high = jnp.maximum(row_block, col_block)
         return jnp.where(row_block == col_block, 1, mask_ref[low, high]).astype(jnp.float32)
 
-    def make_columns(group, carry):
-        columns = uj[pl.ds(2 * group, 2)].reshape(2 * CHUNK, emb_ref.shape[1])
-        col_blocks = [
-            block_of(back(y, core * (2 * group + half)), back(z, (1 - core) * (2 * group + half)))
-            for half in range(2)
-        ]
-        sums = jnp.zeros((1, 2 * CHUNK), jnp.float32)
-        for k in range(SIDE):
-            row_block = block_of(back(y, (1 - core) * k), back(z, core * k))
-            cosine = lax.dot_general(
-                ui[k], columns, (((1,), (1,)), ((), ())), preferred_element_type=jnp.float32
-            )
-            keep = jnp.where(
-                lane < CHUNK, kept(row_block, col_blocks[0]), kept(row_block, col_blocks[1])
-            )
-            weights = jnp.exp2(cosine * scale) * keep
-            if k == 0:
-                own_row = lax.broadcasted_iota(jnp.int32, weights.shape, 0)
-                own_col = lax.broadcasted_iota(jnp.int32, weights.shape, 1) + group * (2 * CHUNK)
-                weights = jnp.where(own_row == own_col, 0.0, weights)
-            weights = weights.astype(jnp.bfloat16)
-            kmat[k, :, pl.ds(pl.multiple_of(group * 2 * CHUNK, 2 * CHUNK), 2 * CHUNK)] = weights
-            sums = sums + jnp.sum(weights.astype(jnp.float32), axis=0, keepdims=True)
-        deg[0, pl.ds(2 * group, 1), :] = sums[:, :CHUNK]
-        deg[0, pl.ds(2 * group + 1, 1), :] = sums[:, CHUNK:]
-        return carry
-
-    lax.fori_loop(0, SIDE // 2, make_columns, 0)
-
+    groups = range(SIDE // 2)
+    col_blocks = [block_of(back(y, core * k), back(z, (1 - core) * k)) for k in range(SIDE)]
+    row_blocks = [block_of(back(y, (1 - core) * k), back(z, core * k)) for k in range(SIDE)]
+
+    def make_tile(vecs, k, group):
+        cosine = lax.dot_general(
+            vecs[k],
+            uj[2 * group : 2 * group + 2].reshape(2 * CHUNK, emb_ref.shape[1]),
+            (((1,), (1,)), ((), ())),
+            preferred_element_type=jnp.float32,
+        )
+        keep = jnp.where(
+            lane < CHUNK,
+            kept(row_blocks[k], col_blocks[2 * group]),
+            kept(row_blocks[k], col_blocks[2 * group + 1]),
+        )
+        weights = jnp.exp2(cosine * scale)
+        if k == 0 and group == 0:
+            own_row = lax.broadcasted_iota(jnp.int32, weights.shape, 0)
+            own_col = lax.broadcasted_iota(jnp.int32, weights.shape, 1)
+            weights = jnp.where(own_row == own_col, 0.0, weights)
+        kmat[k, :, 2 * CHUNK * group : 2 * CHUNK * (group + 1)] = weights.astype(
+            jnp.bfloat16
+        ) * keep.astype(jnp.bfloat16)
+        return jnp.sum(weights, axis=0, keepdims=True) * keep
+
+    load_mask.wait()
+    sums = [make_tile(uj, 0, group) for group in groups]
+    whole(UNIT_PASS, ui.at[others]).wait_recv()
+    for group in groups:
+        for k in range(1, SIDE):
+            sums[group] = sums[group] + make_tile(ui, k, group)
+        deg[0, 2 * group : 2 * group + 1, :] = sums[group][:, :CHUNK]
+        deg[0, 2 * group + 1 : 2 * group + 2, :] = sums[group][:, CHUNK:]
     for k in FAR_FIRST:
         send(DEGREE, deg.at[0], deg.at[k], gather_peer(k))
     whole(LABEL_GATHER, lab.at[others]).wait_recv()
@@ -238,48 +240,58 @@
     def rows_of(half):
         return pl.ds(half * HALF, HALF)
 
-    def iterate(phases, scaled, part, rcv, finish):
-        spreads = []
-        for half in range(2):
-            rows = rows_of(half)
-            spread = jnp.dot(
-                kmat[:, rows, :].reshape(SIDE * HALF, SIDE * CHUNK),
-                scaled[...].reshape(SIDE * CHUNK, LANES),
-                preferred_element_type=jnp.float32,
-            ).reshape(SIDE, HALF, LANES)
-            spreads.append(spread[0])
-            for k in FAR_FIRST:
-                part[k, rows, :] = spread[k].astype(jnp.bfloat16)
-            for k in FAR_FIRST:
-                send(phases[half], part.at[k, rows, :], rcv.at[k, rows, :], reduce_peer(SIDE - k))
-        for half in range(2):
-            whole(phases[half], rcv.at[others, rows_of(half), :]).wait_recv()
-            total = spreads[half]
-            for k in range(1, SIDE):
-                total = total + rcv[k, rows_of(half), :].astype(jnp.float32)
-            rows = slice(half * HALF, (half + 1) * HALF)
-            finish(half, MIXING * own_root[rows] * total + (1.0 - MIXING) * seeds[rows])
-
-    def finish_first(half, current):
+    def spread_half(scaled, part, half):
         rows = rows_of(half)
-        root = own_root[half * HALF : (half + 1) * HALF]
-        sc2[0, rows, :] = (root * current).astype(jnp.bfloat16)
+        spread = jnp.dot(
+            kmat[:, rows, :].reshape(SIDE * HALF, SIDE * CHUNK),
+            scaled[...].reshape(SIDE * CHUNK, LANES),
+            preferred_element_type=jnp.float32,
+        ).reshape(SIDE, HALF, LANES)
+        part[:, rows, :] = spread.astype(jnp.bfloat16)
+        return spread[0]
+
+    spreads = []
+    for half in range(2):
+        rows = rows_of(half)
+        spreads.append(spread_half(sc1, part1, half))
+        for k in FAR_FIRST:
+            send(REDUCE1[half], part1.at[k, rows, :], rcv1.at[k, rows, :], reduce_peer(SIDE - k))
+    root[...] = jnp.broadcast_to(own_root, root.shape)
+    for half in range(2):
+        rows = rows_of(half)
+        picked = slice(half * HALF, (half + 1) * HALF)
+        whole(REDUCE1[half], rcv1.at[others, rows, :]).wait_recv()
+        total = spreads[half]
+        for k in range(1, SIDE):
+            total = total + rcv1[k, rows, :].astype(jnp.float32)
+        current = MIXING * own_root[picked] * total + (1.0 - MIXING) * seeds[picked]
+        sc2[0, rows, :] = (own_root[picked] * current).astype(jnp.bfloat16)
         for k in FAR_FIRST:
             send(GATHER2[half], sc2.at[0, rows, :], sc2.at[k, rows, :], gather_peer(k))
-
-    def finish_last(half, current):
-        fin[rows_of(half), :] = current.astype(jnp.bfloat16)
-
-    iterate(REDUCE1, sc1, part1, rcv1, finish_first)
+    root_wide[...] = jnp.concatenate([root[own_rows, :]] * SIDE, axis=1)
+    store_root = local(STORE_ROOT, root_wide, root_hbm)
     for half in range(2):
         whole(GATHER2[half], sc2.at[others, rows_of(half), :]).wait_recv()
-    iterate(REDUCE2, sc2, part2, rcv2, finish_last)
-    store_own = local(STORE_OWN, fin.at[own_rows, :], out_hbm.at[:, own_lanes])
+    for half in range(2):
+        spread_half(sc2, part2, half)
+        for k in FAR_FIRST:
+            new_row, new_col = reduce_peer(SIDE - k)
+            first = lax.div(new_col, SIDE) * SIDE
+            for member in range(half * SIDE // 2, (half + 1) * SIDE // 2):
+                send(
+                    REDUCE2,
+                    part2.at[k, member * PIECE : (member + 1) * PIECE, :],
+                    parts_hbm.at[k, :, own_lanes],
+                    (new_row, first + member),
+                )
     for k in range(1, SIDE):
         rows = pl.ds(pl.multiple_of(swap_index(k) * PIECE, PIECE), PIECE)
-        send(FINAL, fin.at[rows, :], out_hbm.at[:, own_lanes], swap_peer(k))
-    whole(FINAL, fin.at[0 : (SIDE - 1) * PIECE, :]).wait_recv()
+        send(OWN_REDUCE2, part2.at[0, rows, :], parts_hbm.at[0, :, own_lanes], swap_peer(k))
+    store_own = local(STORE_OWN, part2.at[0, own_rows, :], parts_hbm.at[0, :, own_lanes])
+    store_root.wait()
     store_own.wait()
+    whole(OWN_REDUCE2, rcv1.at[0, 0 : (SIDE - 1) * PIECE, :]).wait_recv()
+    whole(REDUCE2, rcv1.at[others]).wait_recv()
     for copy in sent:
         copy.wait_send()
 
@@ -289,11 +301,14 @@
     anywhere = pl.BlockSpec(memory_space=pl.ANY)
     units = pltpu.VMEM((SIDE, CHUNK, width), jnp.bfloat16)
     chunks = pltpu.VMEM((SIDE, CHUNK, LANES), jnp.bfloat16)
-    return pl.pallas_call(
+    parts, root = pl.pallas_call(
         spread_kernel,
-        out_shape=jax.ShapeDtypeStruct(labels.shape, jnp.bfloat16),
+        out_shape=(
+            jax.ShapeDtypeStruct((SIDE, *labels.shape), jnp.bfloat16),
+            jax.ShapeDtypeStruct(labels.shape, jnp.float32),
+        ),
         in_specs=[anywhere] * 3,
-        out_specs=anywhere,
+        out_specs=(anywhere, anywhere),
         scratch_shapes=[
             pltpu.SMEM(tile_mask.shape, jnp.int32),
             pltpu.VMEM(embeddings.shape, jnp.bfloat16),
@@ -306,15 +321,20 @@
             chunks,
             chunks,
             chunks,
-            chunks,
             pltpu.VMEM((SIDE, SIDE, CHUNK), jnp.float32),
-            pltpu.VMEM((CHUNK, LANES), jnp.bfloat16),
+            pltpu.VMEM((CHUNK, LANES), jnp.float32),
+            pltpu.VMEM(labels.shape, jnp.float32),
             pltpu.SemaphoreType.DMA((PHASES,)),
             pltpu.SemaphoreType.DMA((PHASES + SLOTS,)),
-            pltpu.SemaphoreType.DMA((4,)),
+            pltpu.SemaphoreType.DMA((5,)),
         ],
         compiler_params=pltpu.CompilerParams(collective_id=0, has_side_effects=True),
     )(tile_mask, embeddings, labels)
+    spread = parts[0].astype(jnp.float32)
+    for k in range(1, SIDE):
+        spread = spread + parts[k].astype(jnp.float32)
+    current = MIXING * root * spread + (1.0 - MIXING) * labels.astype(jnp.float32)
+    return current.astype(jnp.bfloat16)
 
 
 def solution(mesh):

time: 57.2 us -> 53.1 us (0.928)
  Pallas kernels: 55.6 us -> 51.2 us
  other arithmetic: 0 us -> 1.59 us
  local copies, waits for them, and re-layouts: 1.38 us -> 0.01 us
    pallas_call x1, Pallas kernels: 55.6 us -> 51.2 us  [shards(): pl.pallas_call(spread_kernel, out_shape=(jax.ShapeDtypeStruct((SIDE, *lab...]
    convert_element_type x0 -> x1, other arithmetic: none -> 1.59 us  [shards(): return current.astype(jnp.bfloat16)]
    unnamed x1 -> x2, local copies, waits for them, and re-layouts: 1.38 us -> 0.01 us
where the time goes in v4:
time: 53.1 us; the launch traced here: 52.9 us
  Pallas kernels  51.2 us (96%)
  other arithmetic  1.59 us (3%)
    pallas_call x1, Pallas kernels, shards(): pl.pallas_call(spread_kernel, out_shape=(jax.ShapeDtypeStruct((SIDE, *lab...  51.2 us
    convert_element_type x1, other arithmetic, shards(): return current.astype(jnp.bfloat16)  1.59 us

profile of v4, /device:TPU:1, one launch (start us, length us, event | category | flops | bytes accessed | tf_op | source)
XLA Modules:
  0.0 52.9 jit_solution(6123453426729818773)
XLA Ops:
  0.0 0.0 copy-start
  0.0 51.2 %shard_map.37 = (bf16[8,16,1024]{2,1,0:T(8,128)(2,1)}, f32[16,1024]{1,0:T(8,128)}) custom-call(s32[32,32]{1,0:T(8,128)} %mask_hbm.1, bf16[16,256]{1,0:T(8,128)(2,1)} %emb_hbm.1, bf16[16,1024]{1,0:T(8,128)(2,1)} %lab_hbm.1), custom_call_target="tpu_custom_call" | custom-call | tf_op jit(solution)/shard_map/pallas_call | solution.py:304
  51.3 0.0 copy-done
  51.3 1.6 %fusion.1 = bf16[16,1024]{1,0:T(8,128)(2,1)} fusion(bf16[16,1024]{1,0:T(8,128)(2,1)S(1)} %copy-done, f32[16,1024]{1,0:T(8,128)} %get-tuple-element.7, bf16[8,16,1024]{2,1,0:T(8,128)(2,1)} %get-tuple-element.8), kind=kLoop, calls=%fused_computation.2 | loop fusion | flops 344064 | bytes 393216 | tf_op jit(solution)/shard_map/convert_element_type | solution.py:337
Async XLA Ops:
  0.0 51.3 %copy-start = (bf16[16,1024]{1,0:T(8,128)(2,1)S(1)}, bf16[16,1024]{1,0:T(8,128)(2,1)}, u32[]{:S(2)}) copy-start(bf16[16,1024]{1,0:T(8,128)(2,1)} %lab_hbm.1) | copy-start | bytes 98308

commit v5 on v4

--- a/solution.py
+++ b/solution.py
@@ -45,6 +45,7 @@
     part1,
     part2,
     rcv1,
+    acc,
     deg,
     root,
     root_wide,
@@ -101,7 +102,7 @@
     load_mask = local(LOAD_MASK, mask_hbm, mask_ref)
     barrier = pltpu.get_barrier_semaphore()
     for k in range(1, SIDE):
-        for peer in (gather_peer(k), reduce_peer(k), swap_peer(k), beside(gather_peer(k))):
+        for peer in (gather_peer(k), swap_peer(k), beside(gather_peer(k))):
             pl.semaphore_signal(barrier, inc=1, device_id=peer, device_id_type=MESH)
 
     def describe(phase, src, dst, device, slot=None):
@@ -132,7 +133,7 @@
     norm = lax.rsqrt(jnp.sum(values * values, axis=1, keepdims=True) + EPSILON)
     uj[0, own_rows, :] = (values * norm).astype(jnp.bfloat16)
 
-    pl.semaphore_wait(barrier, 4 * (SIDE - 1))
+    pl.semaphore_wait(barrier, 3 * (SIDE - 1))
 
     for k in range(1, SIDE):
         send(UNIT_SWAP, uj.at[0, own_rows, low], uj.at[0, own_rows, low], swap_peer(k))
@@ -190,40 +191,55 @@
         high = jnp.maximum(row_block, col_block)
         return jnp.where(row_block == col_block, 1, mask_ref[low, high]).astype(jnp.float32)
 
-    groups = range(SIDE // 2)
     col_blocks = [block_of(back(y, core * k), back(z, (1 - core) * k)) for k in range(SIDE)]
     row_blocks = [block_of(back(y, (1 - core) * k), back(z, core * k)) for k in range(SIDE)]
 
-    def make_tile(vecs, k, group):
+    def kept_lanes(k, quad):
+        bits = [kept(row_blocks[k], col_blocks[4 * quad + j]) for j in range(4)]
+        return jnp.where(
+            lane < 2 * HALF,
+            jnp.where(lane < HALF, bits[0], bits[1]),
+            jnp.where(lane < 3 * HALF, bits[2], bits[3]),
+        )
+
+    def make_tile(vecs, k, half, quad, keep):
         cosine = lax.dot_general(
             vecs[k],
-            uj[2 * group : 2 * group + 2].reshape(2 * CHUNK, emb_ref.shape[1]),
+            uj[4 * quad : 4 * quad + 4, half * HALF : (half + 1) * HALF, :].reshape(
+                4 * HALF, emb_ref.shape[1]
+            ),
             (((1,), (1,)), ((), ())),
             preferred_element_type=jnp.float32,
         )
-        keep = jnp.where(
-            lane < CHUNK,
-            kept(row_blocks[k], col_blocks[2 * group]),
-            kept(row_blocks[k], col_blocks[2 * group + 1]),
-        )
         weights = jnp.exp2(cosine * scale)
-        if k == 0 and group == 0:
+        if k == 0 and quad == 0:
             own_row = lax.broadcasted_iota(jnp.int32, weights.shape, 0)
             own_col = lax.broadcasted_iota(jnp.int32, weights.shape, 1)
-            weights = jnp.where(own_row == own_col, 0.0, weights)
-        kmat[k, :, 2 * CHUNK * group : 2 * CHUNK * (group + 1)] = weights.astype(
+            own = (own_col < HALF) & (own_row == own_col + half * HALF)
+            weights = jnp.where(own, 0.0, weights)
+        start = (2 * half + quad) * 4 * HALF
+        kmat[k, :, start : start + 4 * HALF] = weights.astype(jnp.bfloat16) * keep.astype(
             jnp.bfloat16
-        ) * keep.astype(jnp.bfloat16)
+        )
         return jnp.sum(weights, axis=0, keepdims=True) * keep
 
     load_mask.wait()
-    sums = [make_tile(uj, 0, group) for group in groups]
+    sums = {}
+    for quad in range(2):
+        keep = kept_lanes(0, quad)
+        for half in range(2):
+            sums[half, quad] = make_tile(uj, 0, half, quad, keep)
     whole(UNIT_PASS, ui.at[others]).wait_recv()
-    for group in groups:
-        for k in range(1, SIDE):
-            sums[group] = sums[group] + make_tile(ui, k, group)
-        deg[0, 2 * group : 2 * group + 1, :] = sums[group][:, :CHUNK]
-        deg[0, 2 * group + 1 : 2 * group + 2, :] = sums[group][:, CHUNK:]
+    for quad in range(2):
+        keeps = [kept_lanes(k, quad) for k in range(SIDE)]
+        for half in range(2):
+            for k in range(1, SIDE):
+                sums[half, quad] = sums[half, quad] + make_tile(ui, k, half, quad, keeps[k])
+        for j in range(4):
+            lanes = slice(j * HALF, (j + 1) * HALF)
+            deg[0, 4 * quad + j : 4 * quad + j + 1, :] = jnp.concatenate(
+                [sums[0, quad][:, lanes], sums[1, quad][:, lanes]], axis=1
+            )
     for k in FAR_FIRST:
         send(DEGREE, deg.at[0], deg.at[k], gather_peer(k))
     whole(LABEL_GATHER, lab.at[others]).wait_recv()
@@ -233,27 +249,28 @@
         degree = degree + pltpu.roll(deg[k], k, 0)
     inv_root = jnp.transpose(lax.rsqrt(degree))
     for k in range(SIDE):
-        sc1[k] = (lab[k].astype(jnp.float32) * inv_root[:, k : k + 1]).astype(jnp.bfloat16)
+        scaled = (lab[k].astype(jnp.float32) * inv_root[:, k : k + 1]).astype(jnp.bfloat16)
+        sc1[:, k] = scaled.reshape(2, HALF, LANES)
     own_root = inv_root[:, 0:1]
     seeds = lab[0].astype(jnp.float32)
 
     def rows_of(half):
         return pl.ds(half * HALF, HALF)
 
-    def spread_half(scaled, part, half):
-        rows = rows_of(half)
-        spread = jnp.dot(
-            kmat[:, rows, :].reshape(SIDE * HALF, SIDE * CHUNK),
-            scaled[...].reshape(SIDE * CHUNK, LANES),
+    def product(rows, lanes, scaled):
+        matrix = kmat[:, rows, lanes]
+        return jnp.dot(
+            matrix.reshape(-1, matrix.shape[2]),
+            scaled.reshape(-1, LANES),
             preferred_element_type=jnp.float32,
-        ).reshape(SIDE, HALF, LANES)
-        part[:, rows, :] = spread.astype(jnp.bfloat16)
-        return spread[0]
+        ).reshape(SIDE, -1, LANES)
 
     spreads = []
     for half in range(2):
         rows = rows_of(half)
-        spreads.append(spread_half(sc1, part1, half))
+        spread = product(rows, slice(None), sc1[...])
+        spreads.append(spread[0])
+        part1[:, rows, :] = spread.astype(jnp.bfloat16)
         for k in FAR_FIRST:
             send(REDUCE1[half], part1.at[k, rows, :], rcv1.at[k, rows, :], reduce_peer(SIDE - k))
     root[...] = jnp.broadcast_to(own_root, root.shape)
@@ -265,15 +282,19 @@
         for k in range(1, SIDE):
             total = total + rcv1[k, rows, :].astype(jnp.float32)
         current = MIXING * own_root[picked] * total + (1.0 - MIXING) * seeds[picked]
-        sc2[0, rows, :] = (own_root[picked] * current).astype(jnp.bfloat16)
+        sc2[half, 0] = (own_root[picked] * current).astype(jnp.bfloat16)
         for k in FAR_FIRST:
-            send(GATHER2[half], sc2.at[0, rows, :], sc2.at[k, rows, :], gather_peer(k))
+            send(GATHER2[half], sc2.at[half, 0], sc2.at[half, k], gather_peer(k))
     root_wide[...] = jnp.concatenate([root[own_rows, :]] * SIDE, axis=1)
     store_root = local(STORE_ROOT, root_wide, root_hbm)
+    whole(GATHER2[0], sc2.at[0, others]).wait_recv()
+    first_half, last_half = slice(0, SIDE * HALF), slice(SIDE * HALF, SIDE * CHUNK)
+    acc[...] = product(slice(None), first_half, sc2[0])
+    whole(GATHER2[1], sc2.at[1, others]).wait_recv()
     for half in range(2):
-        whole(GATHER2[half], sc2.at[others, rows_of(half), :]).wait_recv()
-    for half in range(2):
-        spread_half(sc2, part2, half)
+        rows = rows_of(half)
+        spread = acc[:, rows, :] + product(rows, last_half, sc2[1])
+        part2[:, rows, :] = spread.astype(jnp.bfloat16)
         for k in FAR_FIRST:
             new_row, new_col = reduce_peer(SIDE - k)
             first = lax.div(new_col, SIDE) * SIDE
@@ -316,11 +337,12 @@
             units,
             pltpu.VMEM((SIDE, CHUNK, SIDE * CHUNK), jnp.bfloat16),
             chunks,
+            pltpu.VMEM((2, SIDE, HALF, LANES), jnp.bfloat16),
+            pltpu.VMEM((2, SIDE, HALF, LANES), jnp.bfloat16),
             chunks,
             chunks,
             chunks,
-            chunks,
-            chunks,
+            pltpu.VMEM((SIDE, CHUNK, LANES), jnp.float32),
             pltpu.VMEM((SIDE, SIDE, CHUNK), jnp.float32),
             pltpu.VMEM((CHUNK, LANES), jnp.float32),
             pltpu.VMEM(labels.shape, jnp.float32),

time: 53.1 us -> 52.9 us (level)
  no operation moved by 1% of the time
where the time goes in v5:
time: 52.9 us; the launch traced here: 52.6 us
  Pallas kernels  51 us (96%)
  other arithmetic  1.59 us (3%)
    pallas_call x1, Pallas kernels, shards(): pl.pallas_call(spread_kernel, out_shape=(jax.ShapeDtypeStruct((SIDE, *lab...  51 us
    convert_element_type x1, other arithmetic, shards(): return current.astype(jnp.bfloat16)  1.59 us

profile of v5, /device:TPU:1, one launch (start us, length us, event | category | flops | bytes accessed | tf_op | source)
XLA Modules:
  0.0 52.6 jit_solution(13966359481737438350)
XLA Ops:
  0.0 0.0 copy-start
  0.0 51.0 %shard_map.37 = (bf16[8,16,1024]{2,1,0:T(8,128)(2,1)}, f32[16,1024]{1,0:T(8,128)}) custom-call(s32[32,32]{1,0:T(8,128)} %mask_hbm.1, bf16[16,256]{1,0:T(8,128)(2,1)} %emb_hbm.1, bf16[16,1024]{1,0:T(8,128)(2,1)} %lab_hbm.1), custom_call_target="tpu_custom_call" | custom-call | tf_op jit(solution)/shard_map/pallas_call | solution.py:325
  51.0 0.0 copy-done
  51.0 1.6 %fusion.1 = bf16[16,1024]{1,0:T(8,128)(2,1)} fusion(bf16[16,1024]{1,0:T(8,128)(2,1)S(1)} %copy-done, f32[16,1024]{1,0:T(8,128)} %get-tuple-element.7, bf16[8,16,1024]{2,1,0:T(8,128)(2,1)} %get-tuple-element.8), kind=kLoop, calls=%fused_computation.2 | loop fusion | flops 344064 | bytes 393216 | tf_op jit(solution)/shard_map/convert_element_type | solution.py:359
Async XLA Ops:
  0.0 51.0 %copy-start = (bf16[16,1024]{1,0:T(8,128)(2,1)S(1)}, bf16[16,1024]{1,0:T(8,128)(2,1)}, u32[]{:S(2)}) copy-start(bf16[16,1024]{1,0:T(8,128)(2,1)} %lab_hbm.1) | copy-start | bytes 98308

commit v6 on v5

--- a/solution.py
+++ b/solution.py
@@ -24,7 +24,10 @@
 REDUCE1, GATHER2 = (6, 7), (8, 9)
 REDUCE2, OWN_REDUCE2, PIECE_GATHER, CROSS = 10, 11, 12, 13
 PHASES = 14
-SLOTS = SIDE - 1 + 3
+CROSS_SLOT = SIDE - 2
+SWAP_SLOT = SIDE + 2
+PIECE_SLOT = SIDE + 6
+SLOTS = SIDE + 9
 LOAD_UNITS, LOAD_LABELS, LOAD_MASK, STORE_ROOT, STORE_OWN = range(5)
 
 
@@ -135,48 +138,72 @@
 
     pl.semaphore_wait(barrier, 3 * (SIDE - 1))
 
-    for k in range(1, SIDE):
-        send(UNIT_SWAP, uj.at[0, own_rows, low], uj.at[0, own_rows, low], swap_peer(k))
+    own_low = uj.at[0, own_rows, low]
+    for k in (2, 1, 3):
+        for peer in (x_peer(k), (row, z_hi * 8 + swap_index(2 * k) + 1 - 2 * core)):
+            send(UNIT_SWAP, own_low, own_low, peer, slot=SWAP_SLOT + k)
+    send(UNIT_SWAP, own_low, own_low, partner, slot=SWAP_SLOT)
     piece = uj.at[0, own_rows, high]
+    group_of = {0: 0, 1: 0, 7: 0, 2: 1, 6: 1, 3: 2, 5: 2, 4: 2}
     for k in FAR_FIRST:
-        send(PIECE_GATHER, piece, uj.at[k, own_rows, high], gather_peer(k))
-        send(PIECE_GATHER, piece, uj.at[k, own_rows, high], cross_peer(k))
-    send(PIECE_GATHER, piece, piece, partner)
+        for peer in (gather_peer(k), cross_peer(k)):
+            slot = PIECE_SLOT + group_of[k]
+            send(PIECE_GATHER, piece, uj.at[k, own_rows, high], peer, slot=slot)
+    send(PIECE_GATHER, piece, piece, partner, slot=PIECE_SLOT)
     for k in range(1, SIDE):
         lanes = pl.ds(pl.multiple_of(swap_index(k) * LANES, LANES), LANES)
         send(LABEL_SWAP, lab_hbm.at[:, lanes], lab.at[0, own_rows, :], swap_peer(k))
 
     others = slice(1, SIDE)
-    whole(UNIT_SWAP, uj.at[0, 0 : (SIDE - 1) * PIECE, low]).wait_recv()
-    unit_gathers = {
-        k: send(UNIT_GATHER, uj.at[0, :, low], uj.at[k, :, low], gather_peer(k), slot=k - 1)
-        for k in FAR_FIRST
-    }
+    pair = lax.div(c, 2) * 2 * PIECE
+
+    def pair_rows(k):
+        start = lax.rem(pair + (4 - k) * 2 * PIECE, CHUNK)
+        return pl.ds(pl.multiple_of(start, 2 * PIECE), 2 * PIECE)
+
+    def gather_pair(x_back):
+        count = 1 if x_back == 0 else 2
+        region = uj.at[0, 0 : count * PIECE, low]
+        describe(UNIT_SWAP, region, region, partner, slot=SWAP_SLOT + x_back).wait_recv()
+        rows = pair_rows(x_back)
+        for k in FAR_FIRST:
+            send(UNIT_GATHER, uj.at[0, rows, low], uj.at[k, rows, low], gather_peer(k), slot=k - 1)
+
+    def cross_group(group, count, slots):
+        region = uj.at[0, 0 : count * PIECE, low]
+        describe(PIECE_GATHER, region, region, partner, slot=PIECE_SLOT + group).wait_recv()
+        for first, last in slots:
+            block = uj.at[first:last, pair_rows(0), high]
+            for k in (2, 1, 3):
+                send(CROSS, block, block, x_peer(k), slot=CROSS_SLOT + k)
+
+    def pass_pair(k):
+        block = uj.at[others, pair_rows(k), high]
+        send(UNIT_PASS, block, ui.at[others, pair_rows(k), high], partner)
+
+    gather_pair(0)
+    gather_pair(1)
+    gather_pair(3)
+    cross_group(0, 5, ((0, 2), (7, 8)))
+    gather_pair(2)
+    cross_group(1, 4, ((2, 3), (6, 7)))
+    cross_group(2, 6, ((3, 6),))
+    whole(UNIT_SWAP, uj.at[0, 0 : (SIDE - 1) * PIECE, low])
     whole(UNIT_GATHER, uj.at[others, :, low])
-    whole(PIECE_GATHER, uj.at[0:5, 0 : 3 * PIECE, low]).wait_recv()
-    pair = lax.div(c, 2) * 2 * PIECE
-
-    def pair_rows(start):
-        return pl.ds(pl.multiple_of(start, 2 * PIECE), 2 * PIECE)
-
-    block = uj.at[:, pair_rows(pair), high]
-    crosses = {k: send(CROSS, block, block, x_peer(k), slot=SIDE - 2 + k) for k in (2, 1, 3)}
+    whole(PIECE_GATHER, uj.at[0:5, 0 : 3 * PIECE, low])
     whole(CROSS, uj.at[:, 0 : 6 * PIECE, high])
-
-    def pass_pair(start):
-        send(UNIT_PASS, uj.at[others, pair_rows(start), high], ui.at[others, pair_rows(start), high], partner)
-
-    pass_pair(pair)
+    pass_pair(0)
     load_labels.wait()
     whole(LABEL_SWAP, lab.at[0, 0 : (SIDE - 1) * PIECE, :]).wait_recv()
     for k in FAR_FIRST:
         send(LABEL_GATHER, lab.at[0], lab.at[k], gather_peer(k))
     for k in NEAR_FIRST:
-        unit_gathers[k].wait_recv()
+        describe(UNIT_GATHER, uj.at[k, :, low], uj.at[k, :, low], partner, slot=k - 1).wait_recv()
         send(UNIT_PASS, uj.at[k, :, low], ui.at[k, :, low], partner)
     for k in (1, 3, 2):
-        crosses[k].wait_recv()
-        pass_pair(lax.rem(pair + (4 - k) * 2 * PIECE, CHUNK))
+        block = uj.at[:, pair_rows(k), high]
+        describe(CROSS, block, block, partner, slot=CROSS_SLOT + k).wait_recv()
+        pass_pair(k)
     scale = SHARPNESS * math.sqrt(emb_ref.shape[1]) * math.log2(math.e)
     lane = lax.broadcasted_iota(jnp.int32, (1, 2 * CHUNK), 1)
 

time: 52.9 us -> 52.2 us (0.987)
  Pallas kernels: 51 us -> 50.2 us
    pallas_call x1, Pallas kernels: 51 us -> 50.2 us  [shards(): pl.pallas_call(spread_kernel, out_shape=(jax.ShapeDtypeStruct((SIDE, *lab...]
where the time goes in v6:
time: 52.2 us; the launch traced here: 51.8 us
  Pallas kernels  50.2 us (96%)
  other arithmetic  1.59 us (3%)
    pallas_call x1, Pallas kernels, shards(): pl.pallas_call(spread_kernel, out_shape=(jax.ShapeDtypeStruct((SIDE, *lab...  50.2 us
    convert_element_type x1, other arithmetic, shards(): return current.astype(jnp.bfloat16)  1.59 us

profile of v6, /device:TPU:1, one launch (start us, length us, event | category | flops | bytes accessed | tf_op | source)
XLA Modules:
  0.0 51.8 jit_solution(16384369453427289657)
XLA Ops:
  0.0 0.0 copy-start
  0.0 50.2 %shard_map.37 = (bf16[8,16,1024]{2,1,0:T(8,128)(2,1)}, f32[16,1024]{1,0:T(8,128)}) custom-call(s32[32,32]{1,0:T(8,128)} %mask_hbm.1, bf16[16,256]{1,0:T(8,128)(2,1)} %emb_hbm.1, bf16[16,1024]{1,0:T(8,128)(2,1)} %lab_hbm.1), custom_call_target="tpu_custom_call" | custom-call | tf_op jit(solution)/shard_map/pallas_call | solution.py:352
  50.2 0.0 copy-done
  50.2 1.6 %fusion.1 = bf16[16,1024]{1,0:T(8,128)(2,1)} fusion(bf16[16,1024]{1,0:T(8,128)(2,1)S(1)} %copy-done, f32[16,1024]{1,0:T(8,128)} %get-tuple-element.7, bf16[8,16,1024]{2,1,0:T(8,128)(2,1)} %get-tuple-element.8), kind=kLoop, calls=%fused_computation.2 | loop fusion | flops 344064 | bytes 393216 | tf_op jit(solution)/shard_map/convert_element_type | solution.py:386
Async XLA Ops:
  0.0 50.2 %copy-start = (bf16[16,1024]{1,0:T(8,128)(2,1)S(1)}, bf16[16,1024]{1,0:T(8,128)(2,1)}, u32[]{:S(2)}) copy-start(bf16[16,1024]{1,0:T(8,128)(2,1)} %lab_hbm.1) | copy-start | bytes 98308

commit v7 on v6

--- a/solution.py
+++ b/solution.py
@@ -20,10 +20,11 @@
 NEAR_FIRST = (1, 7, 2, 6, 3, 5, 4)
 
 HALF = CHUNK // 2
-UNIT_SWAP, LABEL_SWAP, UNIT_GATHER, UNIT_PASS, LABEL_GATHER, DEGREE = range(6)
+UNIT_SWAP, LABEL_SWAP, UNIT_GATHER, UNIT_PASS, LABEL_GATHER = range(5)
 REDUCE1, GATHER2 = (6, 7), (8, 9)
 REDUCE2, OWN_REDUCE2, PIECE_GATHER, CROSS = 10, 11, 12, 13
-PHASES = 14
+DEGREE = (5, 14)
+PHASES = 15
 CROSS_SLOT = SIDE - 2
 SWAP_SLOT = SIDE + 2
 PIECE_SLOT = SIDE + 6
@@ -104,8 +105,8 @@
     load_labels = local(LOAD_LABELS, lab_hbm.at[:, own_lanes], lab.at[0, own_rows, :])
     load_mask = local(LOAD_MASK, mask_hbm, mask_ref)
     barrier = pltpu.get_barrier_semaphore()
-    for k in range(1, SIDE):
-        for peer in (gather_peer(k), swap_peer(k), beside(gather_peer(k))):
+    for k in FAR_FIRST:
+        for peer in (gather_peer(k), beside(gather_peer(k)), swap_peer(k)):
             pl.semaphore_signal(barrier, inc=1, device_id=peer, device_id_type=MESH)
 
     def describe(phase, src, dst, device, slot=None):
@@ -257,29 +258,32 @@
         for half in range(2):
             sums[half, quad] = make_tile(uj, 0, half, quad, keep)
     whole(UNIT_PASS, ui.at[others]).wait_recv()
-    for quad in range(2):
-        keeps = [kept_lanes(k, quad) for k in range(SIDE)]
-        for half in range(2):
+    keeps = [[kept_lanes(k, quad) for k in range(SIDE)] for quad in range(2)]
+    for half in range(2):
+        for quad in range(2):
+            total = sums[half, quad]
             for k in range(1, SIDE):
-                sums[half, quad] = sums[half, quad] + make_tile(ui, k, half, quad, keeps[k])
-        for j in range(4):
-            lanes = slice(j * HALF, (j + 1) * HALF)
-            deg[0, 4 * quad + j : 4 * quad + j + 1, :] = jnp.concatenate(
-                [sums[0, quad][:, lanes], sums[1, quad][:, lanes]], axis=1
-            )
-    for k in FAR_FIRST:
-        send(DEGREE, deg.at[0], deg.at[k], gather_peer(k))
+                total = total + make_tile(ui, k, half, quad, keeps[quad][k])
+            for j in range(4):
+                degrees = total[:, j * HALF : (j + 1) * HALF]
+                deg[half, 0, 4 * quad + j : 4 * quad + j + 1, :] = jnp.concatenate(
+                    [degrees, degrees], axis=1
+                )
+        for k in FAR_FIRST:
+            send(DEGREE[half], deg.at[half, 0], deg.at[half, k], gather_peer(k))
     whole(LABEL_GATHER, lab.at[others]).wait_recv()
-    whole(DEGREE, deg.at[others]).wait_recv()
-    degree = deg[0]
-    for k in range(1, SIDE):
-        degree = degree + pltpu.roll(deg[k], k, 0)
-    inv_root = jnp.transpose(lax.rsqrt(degree))
-    for k in range(SIDE):
-        scaled = (lab[k].astype(jnp.float32) * inv_root[:, k : k + 1]).astype(jnp.bfloat16)
-        sc1[:, k] = scaled.reshape(2, HALF, LANES)
-    own_root = inv_root[:, 0:1]
     seeds = lab[0].astype(jnp.float32)
+
+    def scale_half(half):
+        whole(DEGREE[half], deg.at[half, others]).wait_recv()
+        degree = deg[half, 0]
+        for k in range(1, SIDE):
+            degree = degree + pltpu.roll(deg[half, k], k, 0)
+        inv_root = jnp.transpose(lax.rsqrt(degree))[:HALF]
+        for k in range(SIDE):
+            values = lab[k, half * HALF : (half + 1) * HALF, :].astype(jnp.float32)
+            sc1[half, k] = (values * inv_root[:, k : k + 1]).astype(jnp.bfloat16)
+        return inv_root[:, 0:1]
 
     def rows_of(half):
         return pl.ds(half * HALF, HALF)
@@ -292,14 +296,19 @@
             preferred_element_type=jnp.float32,
         ).reshape(SIDE, -1, LANES)
 
+    first_half, last_half = slice(0, SIDE * HALF), slice(SIDE * HALF, SIDE * CHUNK)
+    own_roots = [scale_half(0)]
+    acc[...] = product(slice(None), first_half, sc1[0])
+    own_roots.append(scale_half(1))
     spreads = []
     for half in range(2):
         rows = rows_of(half)
-        spread = product(rows, slice(None), sc1[...])
+        spread = acc[:, rows, :] + product(rows, last_half, sc1[1])
         spreads.append(spread[0])
         part1[:, rows, :] = spread.astype(jnp.bfloat16)
         for k in FAR_FIRST:
             send(REDUCE1[half], part1.at[k, rows, :], rcv1.at[k, rows, :], reduce_peer(SIDE - k))
+    own_root = jnp.concatenate(own_roots, axis=0)
     root[...] = jnp.broadcast_to(own_root, root.shape)
     for half in range(2):
         rows = rows_of(half)
@@ -315,7 +324,6 @@
     root_wide[...] = jnp.concatenate([root[own_rows, :]] * SIDE, axis=1)
     store_root = local(STORE_ROOT, root_wide, root_hbm)
     whole(GATHER2[0], sc2.at[0, others]).wait_recv()
-    first_half, last_half = slice(0, SIDE * HALF), slice(SIDE * HALF, SIDE * CHUNK)
     acc[...] = product(slice(None), first_half, sc2[0])
     whole(GATHER2[1], sc2.at[1, others]).wait_recv()
     for half in range(2):
@@ -370,7 +378,7 @@
             chunks,
             chunks,
             pltpu.VMEM((SIDE, CHUNK, LANES), jnp.float32),
-            pltpu.VMEM((SIDE, SIDE, CHUNK), jnp.float32),
+            pltpu.VMEM((2, SIDE, SIDE, CHUNK), jnp.float32),
             pltpu.VMEM((CHUNK, LANES), jnp.float32),
             pltpu.VMEM(labels.shape, jnp.float32),
             pltpu.SemaphoreType.DMA((PHASES,)),

time: 52.2 us -> 51.9 us (level)
  no operation moved by 1% of the time
where the time goes in v7:
time: 51.9 us; the launch traced here: 51.7 us
  Pallas kernels  50.1 us (97%)
  other arithmetic  1.59 us (3%)
    pallas_call x1, Pallas kernels, shards(): pl.pallas_call(spread_kernel, out_shape=(jax.ShapeDtypeStruct((SIDE, *lab...  50.1 us
    convert_element_type x1, other arithmetic, shards(): return current.astype(jnp.bfloat16)  1.59 us

profile of v7, /device:TPU:1, one launch (start us, length us, event | category | flops | bytes accessed | tf_op | source)
XLA Modules:
  0.0 51.7 jit_solution(15562146160385498677)
XLA Ops:
  0.0 0.0 copy-start
  0.0 50.1 %shard_map.37 = (bf16[8,16,1024]{2,1,0:T(8,128)(2,1)}, f32[16,1024]{1,0:T(8,128)}) custom-call(s32[32,32]{1,0:T(8,128)} %mask_hbm.1, bf16[16,256]{1,0:T(8,128)(2,1)} %emb_hbm.1, bf16[16,1024]{1,0:T(8,128)(2,1)} %lab_hbm.1), custom_call_target="tpu_custom_call" | custom-call | tf_op jit(solution)/shard_map/pallas_call | solution.py:360
  50.1 0.0 copy-done
  50.1 1.6 %fusion.1 = bf16[16,1024]{1,0:T(8,128)(2,1)} fusion(bf16[16,1024]{1,0:T(8,128)(2,1)S(1)} %copy-done, f32[16,1024]{1,0:T(8,128)} %get-tuple-element.7, bf16[8,16,1024]{2,1,0:T(8,128)(2,1)} %get-tuple-element.8), kind=kLoop, calls=%fused_computation.2 | loop fusion | flops 344064 | bytes 393216 | tf_op jit(solution)/shard_map/convert_element_type | solution.py:394
Async XLA Ops:
  0.0 50.1 %copy-start = (bf16[16,1024]{1,0:T(8,128)(2,1)S(1)}, bf16[16,1024]{1,0:T(8,128)(2,1)}, u32[]{:S(2)}) copy-start(bf16[16,1024]{1,0:T(8,128)(2,1)} %lab_hbm.1) | copy-start | bytes 98308

commit v8 on v7

--- a/solution.py
+++ b/solution.py
@@ -21,10 +21,11 @@
 
 HALF = CHUNK // 2
 UNIT_SWAP, LABEL_SWAP, UNIT_GATHER, UNIT_PASS, LABEL_GATHER = range(5)
-REDUCE1, GATHER2 = (6, 7), (8, 9)
+REDUCE1, GATHER2 = (6, 7, 15, 16), (8, 9)
 REDUCE2, OWN_REDUCE2, PIECE_GATHER, CROSS = 10, 11, 12, 13
 DEGREE = (5, 14)
-PHASES = 15
+PHASES = 17
+QUARTER = HALF // 2
 CROSS_SLOT = SIDE - 2
 SWAP_SLOT = SIDE + 2
 PIECE_SLOT = SIDE + 6
@@ -306,21 +307,26 @@
         spread = acc[:, rows, :] + product(rows, last_half, sc1[1])
         spreads.append(spread[0])
         part1[:, rows, :] = spread.astype(jnp.bfloat16)
-        for k in FAR_FIRST:
-            send(REDUCE1[half], part1.at[k, rows, :], rcv1.at[k, rows, :], reduce_peer(SIDE - k))
+        for quarter in (2 * half, 2 * half + 1):
+            rows = pl.ds(quarter * QUARTER, QUARTER)
+            for k in FAR_FIRST:
+                part = part1.at[k, rows, :]
+                send(REDUCE1[quarter], part, rcv1.at[k, rows, :], reduce_peer(SIDE - k))
     own_root = jnp.concatenate(own_roots, axis=0)
     root[...] = jnp.broadcast_to(own_root, root.shape)
-    for half in range(2):
-        rows = rows_of(half)
-        picked = slice(half * HALF, (half + 1) * HALF)
-        whole(REDUCE1[half], rcv1.at[others, rows, :]).wait_recv()
-        total = spreads[half]
+    for quarter in range(4):
+        half, inner = quarter // 2, quarter % 2 * QUARTER
+        rows = pl.ds(quarter * QUARTER, QUARTER)
+        picked = slice(quarter * QUARTER, (quarter + 1) * QUARTER)
+        whole(REDUCE1[quarter], rcv1.at[others, rows, :]).wait_recv()
+        total = spreads[half][inner : inner + QUARTER]
         for k in range(1, SIDE):
             total = total + rcv1[k, rows, :].astype(jnp.float32)
         current = MIXING * own_root[picked] * total + (1.0 - MIXING) * seeds[picked]
-        sc2[half, 0] = (own_root[picked] * current).astype(jnp.bfloat16)
+        rows = pl.ds(inner, QUARTER)
+        sc2[half, 0, rows, :] = (own_root[picked] * current).astype(jnp.bfloat16)
         for k in FAR_FIRST:
-            send(GATHER2[half], sc2.at[half, 0], sc2.at[half, k], gather_peer(k))
+            send(GATHER2[half], sc2.at[half, 0, rows, :], sc2.at[half, k, rows, :], gather_peer(k))
     root_wide[...] = jnp.concatenate([root[own_rows, :]] * SIDE, axis=1)
     store_root = local(STORE_ROOT, root_wide, root_hbm)
     whole(GATHER2[0], sc2.at[0, others]).wait_recv()

time: 51.9 us -> 52.2 us (level); the launches traced: 51.7 us -> 51.4 us
  no operation moved by 1% of the time
where the time goes in v8:
time: 52.2 us; the launch traced here: 51.4 us
  Pallas kernels  49.8 us (95%)
  other arithmetic  1.59 us (3%)
    pallas_call x1, Pallas kernels, shards(): pl.pallas_call(spread_kernel, out_shape=(jax.ShapeDtypeStruct((SIDE, *lab...  49.8 us
    convert_element_type x1, other arithmetic, shards(): return current.astype(jnp.bfloat16)  1.59 us

profile of v8, /device:TPU:1, one launch (start us, length us, event | category | flops | bytes accessed | tf_op | source)
XLA Modules:
  0.0 51.4 jit_solution(7834403720425228361)
XLA Ops:
  0.0 0.0 copy-start
  0.0 49.8 %shard_map.37 = (bf16[8,16,1024]{2,1,0:T(8,128)(2,1)}, f32[16,1024]{1,0:T(8,128)}) custom-call(s32[32,32]{1,0:T(8,128)} %mask_hbm.1, bf16[16,256]{1,0:T(8,128)(2,1)} %emb_hbm.1, bf16[16,1024]{1,0:T(8,128)(2,1)} %lab_hbm.1), custom_call_target="tpu_custom_call" | custom-call | tf_op jit(solution)/shard_map/pallas_call | solution.py:366
  49.8 0.0 copy-done
  49.8 1.6 %fusion.1 = bf16[16,1024]{1,0:T(8,128)(2,1)} fusion(bf16[16,1024]{1,0:T(8,128)(2,1)S(1)} %copy-done, f32[16,1024]{1,0:T(8,128)} %get-tuple-element.7, bf16[8,16,1024]{2,1,0:T(8,128)(2,1)} %get-tuple-element.8), kind=kLoop, calls=%fused_computation.2 | loop fusion | flops 344064 | bytes 393216 | tf_op jit(solution)/shard_map/convert_element_type | solution.py:400
Async XLA Ops:
  0.0 49.8 %copy-start = (bf16[16,1024]{1,0:T(8,128)(2,1)S(1)}, bf16[16,1024]{1,0:T(8,128)(2,1)}, u32[]{:S(2)}) copy-start(bf16[16,1024]{1,0:T(8,128)(2,1)} %lab_hbm.1) | copy-start | bytes 98308

commit v9 on v7

--- a/solution.py
+++ b/solution.py
@@ -145,7 +145,7 @@
             send(UNIT_SWAP, own_low, own_low, peer, slot=SWAP_SLOT + k)
     send(UNIT_SWAP, own_low, own_low, partner, slot=SWAP_SLOT)
     piece = uj.at[0, own_rows, high]
-    group_of = {0: 0, 1: 0, 7: 0, 2: 1, 6: 1, 3: 2, 5: 2, 4: 2}
+    group_of = {0: 0, 1: 0, 7: 0, 2: 1, 6: 1, 3: 1, 5: 1, 4: 1}
     for k in FAR_FIRST:
         for peer in (gather_peer(k), cross_peer(k)):
             slot = PIECE_SLOT + group_of[k]
@@ -171,7 +171,7 @@
             send(UNIT_GATHER, uj.at[0, rows, low], uj.at[k, rows, low], gather_peer(k), slot=k - 1)
 
     def cross_group(group, count, slots):
-        region = uj.at[0, 0 : count * PIECE, low]
+        region = uj.at[0 : count // 5, 0 : 5 * PIECE, low]
         describe(PIECE_GATHER, region, region, partner, slot=PIECE_SLOT + group).wait_recv()
         for first, last in slots:
             block = uj.at[first:last, pair_rows(0), high]
@@ -187,8 +187,7 @@
     gather_pair(3)
     cross_group(0, 5, ((0, 2), (7, 8)))
     gather_pair(2)
-    cross_group(1, 4, ((2, 3), (6, 7)))
-    cross_group(2, 6, ((3, 6),))
+    cross_group(1, 10, ((2, 7),))
     whole(UNIT_SWAP, uj.at[0, 0 : (SIDE - 1) * PIECE, low])
     whole(UNIT_GATHER, uj.at[others, :, low])
     whole(PIECE_GATHER, uj.at[0:5, 0 : 3 * PIECE, low])

time: 51.9 us -> 51.8 us (level)
  no operation moved by 1% of the time
where the time goes in v9:
time: 51.8 us; the launch traced here: 51.4 us
  Pallas kernels  49.8 us (96%)
  other arithmetic  1.59 us (3%)
    pallas_call x1, Pallas kernels, shards(): pl.pallas_call(spread_kernel, out_shape=(jax.ShapeDtypeStruct((SIDE, *lab...  49.8 us
    convert_element_type x1, other arithmetic, shards(): return current.astype(jnp.bfloat16)  1.59 us

profile of v9, /device:TPU:1, one launch (start us, length us, event | category | flops | bytes accessed | tf_op | source)
XLA Modules:
  0.0 51.4 jit_solution(5569344133976849829)
XLA Ops:
  0.0 0.0 copy-start
  0.0 49.8 %shard_map.37 = (bf16[8,16,1024]{2,1,0:T(8,128)(2,1)}, f32[16,1024]{1,0:T(8,128)}) custom-call(s32[32,32]{1,0:T(8,128)} %mask_hbm.1, bf16[16,256]{1,0:T(8,128)(2,1)} %emb_hbm.1, bf16[16,1024]{1,0:T(8,128)(2,1)} %lab_hbm.1), custom_call_target="tpu_custom_call" | custom-call | tf_op jit(solution)/shard_map/pallas_call | solution.py:359
  49.8 0.0 copy-done
  49.8 1.6 %fusion.1 = bf16[16,1024]{1,0:T(8,128)(2,1)} fusion(bf16[16,1024]{1,0:T(8,128)(2,1)S(1)} %copy-done, f32[16,1024]{1,0:T(8,128)} %get-tuple-element.7, bf16[8,16,1024]{2,1,0:T(8,128)(2,1)} %get-tuple-element.8), kind=kLoop, calls=%fused_computation.2 | loop fusion | flops 344064 | bytes 393216 | tf_op jit(solution)/shard_map/convert_element_type | solution.py:393
Async XLA Ops:
  0.0 49.8 %copy-start = (bf16[16,1024]{1,0:T(8,128)(2,1)S(1)}, bf16[16,1024]{1,0:T(8,128)(2,1)}, u32[]{:S(2)}) copy-start(bf16[16,1024]{1,0:T(8,128)(2,1)} %lab_hbm.1) | copy-start | bytes 98308
